TPU v7x, 32 devices: a whole 2x2x4 slice. The times are simulated.
32 devices in a mesh: dp: 4 (over z), seq: 2 (over y), tensor: 4 (over x, core).
Axes of the slice: x: 2, y: 2, z: 4, core: 2. Of those that a mesh axis runs over, the one named last changes fastest.
Arguments:
- patch_states: bfloat16 [4, 768, 4096], P('dp', 'seq', 'tensor'), may hold values from -6 to 6
- residual_grad: bfloat16 [4, 768, 4096], P('dp', 'seq', 'tensor'), may hold values from -3 to 3
- upstream_value: bfloat16 [4, 768, 512], P('dp', 'seq'), may hold values from -6 to 6
- norm_gain: bfloat16 [4096], P('tensor'), may hold values from 0.099609375 to 1.8984375
- value_weight: bfloat16 [512, 4096], P(('dp', 'seq'), 'tensor'), may hold values from -0.09375 to 0.09375
- out_weight: bfloat16 [512, 4096], P(('dp', 'seq'), 'tensor'), may hold values from -0.25 to 0.25
- attn_out: bfloat16 [4, 768, 512], P('dp', 'seq'), may hold values from -6 to 6
- queries: bfloat16 [4, 768, 512], P('dp', 'seq', 'tensor'), may hold values from -1.5 to 1.5
- byte_keys: bfloat16 [4, 16384, 512], P('dp', 'seq', 'tensor'), may hold values from -1.5 to 1.5
- byte_values: bfloat16 [4, 16384, 512], P('dp', 'seq', 'tensor'), may hold values from -6 to 6
- patch_starts: int32 [4, 768], P('dp'), may hold values from 0 to 16383, as said below
Outputs:
- wgrad_value: float32 [512, 4096], P(('dp', 'seq'), 'tensor')
- wgrad_out: float32 [512, 4096], P(('dp', 'seq'), 'tensor')
- grad_keys: bfloat16 [4, 16384, 512], P('dp', 'seq', 'tensor')
- grad_values: bfloat16 [4, 16384, 512], P('dp', 'seq', 'tensor')
Inputs may be any that keep to these rules, and one draw needn't show every extreme that they name: `patch_starts`: row i lists, increasing, the first byte of each of the 768 patches of sequence i. Every multiple of 8192 is among them, so no patch crosses the boundary between two byte shards. In every sequence one byte shard holds 768 patches, or 767 where that is fewer, and no byte shard holds more. The bytes of patch j lie on byte shard j // 384 - 1, j // 384 or j // 384 + 1.
All inputs are finite; a program needn't handle non-finite values.
Results may differ from a plain program's by a relative error of at most 0.0058.
Values may be sent and summed in bfloat16 or wider, within the bound.
A program may use at most 128 MiB of HBM per device.

v0:
```python
import functools
import math

import jax
import jax.numpy as jnp
from jax import lax
from jax.experimental import pallas as pl
from jax.experimental.pallas import tpu as pltpu
from jax.sharding import PartitionSpec as P

HD = 128


def member_sum(member32, terms):
    return lax.dot_general(
        member32,
        terms,
        (((0,), (0,)), ((), ())),
        precision=lax.Precision.HIGHEST,
        preferred_element_type=jnp.float32,
    )


def member_spread(member32, totals):
    return jnp.dot(
        member32, totals, precision=lax.Precision.HIGHEST, preferred_element_type=jnp.float32
    )


def cross_backward(member, segment_rows, keys, values, head_width):
    nbytes = keys.shape[0]
    heads = keys.shape[1] // HD
    scale = 1.0 / math.sqrt(HD)
    member32 = member.astype(jnp.float32)
    picked = jnp.dot(member, segment_rows, preferred_element_type=jnp.float32).astype(jnp.bfloat16)
    grad_f = picked[:, :head_width].astype(jnp.float32).reshape(nbytes, heads, HD)
    query_f = picked[:, head_width:].astype(jnp.float32).reshape(nbytes, heads, HD)
    keys_f = keys.astype(jnp.float32).reshape(nbytes, heads, HD)
    values_f = values.astype(jnp.float32).reshape(nbytes, heads, HD)
    scores = jnp.sum(query_f * keys_f, axis=-1) * scale
    expo = jnp.exp(scores)
    totals = member_spread(member32, member_sum(member32, expo))
    probs = expo / totals
    grad_values = (probs[..., None] * grad_f).reshape(nbytes, heads * HD).astype(jnp.bfloat16)
    prob_grad = jnp.sum(grad_f * values_f, axis=-1)
    mass = member_spread(member32, member_sum(member32, probs * prob_grad))
    score_grad = probs * (prob_grad - mass)
    grad_keys = (
        (score_grad[..., None] * query_f * scale).reshape(nbytes, heads * HD).astype(jnp.bfloat16)
    )
    return (grad_keys, grad_values)


def contract_rows(left, right):
    return lax.dot_general(
        left, right, (((0,), (0,)), ((), ())), preferred_element_type=jnp.float32
    )


def on_device(
    patch_states,
    residual_grad,
    upstream_value,
    norm_gain,
    value_weight,
    out_weight,
    attn_out,
    queries,
    byte_keys,
    byte_values,
    patch_starts,
):
    states = patch_states[0]
    patches = states.shape[0]
    width_local = states.shape[1]
    model_width = width_local * lax.axis_size("tensor")
    states32 = states.astype(jnp.float32)
    gain32 = norm_gain.astype(jnp.float32)
    upstream = upstream_value[0]
    context = attn_out[0]
    value_full, out_full = (
        lax.all_gather(value_weight, ("dp", "seq"), axis=0, tiled=True),
        lax.all_gather(out_weight, ("dp", "seq"), axis=0, tiled=True),
    )
    grad_normed = jnp.dot(upstream, value_full, preferred_element_type=jnp.float32)
    square_part = jnp.sum(states32 * states32, axis=1)
    cross_part = jnp.sum(grad_normed * gain32 * states32, axis=1)
    square_sum, cross_sum = lax.psum((square_part, cross_part), "tensor")
    inv_rms = lax.rsqrt(square_sum / model_width + 1e-05)
    normed = (states32 * inv_rms[:, None] * gain32).astype(jnp.bfloat16)
    grad_patch = (
        residual_grad[0].astype(jnp.float32)
        + inv_rms[:, None] * gain32 * grad_normed
        - (inv_rms**3)[:, None] * states32 * (cross_sum / model_width)[:, None]
    ).astype(jnp.bfloat16)
    partial_attn = lax.dot_general(
        grad_patch, out_full, (((1,), (1,)), ((), ())), preferred_element_type=jnp.float32
    )
    columns = upstream
    wgrad_value = lax.psum_scatter(
        contract_rows(columns, normed), ("dp", "seq"), scatter_dimension=0, tiled=True
    )
    columns = context
    wgrad_out = lax.psum_scatter(
        contract_rows(columns, grad_patch), ("dp", "seq"), scatter_dimension=0, tiled=True
    )
    attn_all = lax.psum(partial_attn, "tensor").astype(jnp.bfloat16)
    head_width = queries.shape[2]
    grad_attn = lax.dynamic_slice_in_dim(
        attn_all, lax.axis_index("tensor") * head_width, head_width, 1
    )
    starts = patch_starts[0]
    total_patches = starts.shape[0]
    seq_count = lax.axis_size("seq")
    seq_pos = lax.axis_index("seq")
    byte_count = byte_keys.shape[1]
    window_len = 2 * patches
    owners = starts // byte_count
    shard_ids = jnp.arange(seq_count, dtype=jnp.int32)
    firsts = jnp.sum((owners[None, :] < shard_ids[:, None]).astype(jnp.int32), axis=1)
    my_first = jnp.sum(firsts * (shard_ids == seq_pos).astype(jnp.int32))
    payload = jnp.concatenate([grad_attn, queries[0]], axis=1)
    padded_starts = jnp.concatenate(
        [starts, jnp.full((window_len,), 2 * total_patches * byte_count + byte_count, jnp.int32)]
    )
    local_starts = lax.dynamic_slice_in_dim(padded_starts, my_first, window_len)
    positions = seq_pos * byte_count + jnp.arange(byte_count, dtype=jnp.int32)
    reached = local_starts[None, :] <= positions[:, None]
    after = jnp.concatenate([reached[:, 1:], jnp.zeros((byte_count, 1), bool)], axis=1)
    member = (reached & jnp.logical_not(after)).astype(jnp.bfloat16)
    mine = seq_pos * patches + jnp.arange(patches, dtype=jnp.int32)
    targets = lax.dynamic_slice_in_dim(owners, seq_pos * patches, patches)
    target_first = jnp.sum((owners[None, :] < targets[:, None]).astype(jnp.int32), axis=1)
    slots = mine - jnp.maximum(seq_pos * patches, target_first)
    dest = targets * patches + slots
    place = (jnp.arange(seq_count * patches, dtype=jnp.int32)[:, None] == dest[None, :]).astype(
        jnp.bfloat16
    )
    outgoing = jnp.dot(place, payload, preferred_element_type=jnp.float32).astype(jnp.bfloat16)
    outgoing = outgoing.reshape(seq_count, patches, 2 * head_width)
    incoming = lax.all_to_all(outgoing, "seq", split_axis=0, concat_axis=0, tiled=True)
    wanted = my_first + jnp.arange(window_len, dtype=jnp.int32)
    sources = wanted // patches
    received_row = sources * patches + wanted - jnp.maximum(sources * patches, my_first)
    select = (
        received_row[:, None] == jnp.arange(seq_count * patches, dtype=jnp.int32)[None, :]
    ).astype(jnp.bfloat16)
    segment_rows = jnp.dot(
        select,
        incoming.reshape(seq_count * patches, 2 * head_width),
        preferred_element_type=jnp.float32,
    ).astype(jnp.bfloat16)
    grad_keys, grad_values = cross_backward(
        member, segment_rows, byte_keys[0], byte_values[0], head_width
    )
    return (wgrad_value, wgrad_out, grad_keys[None], grad_values[None])


def split3(x):
    hi = x.astype(jnp.bfloat16).astype(jnp.float32)
    rest = x - hi
    mid = rest.astype(jnp.bfloat16).astype(jnp.float32)
    return hi, mid, rest - mid


def byte_sums(block, scale, first, last, bounds, rows, keys, values, member, picked, expo, pgrad, sums):
    width = bounds.shape[1]
    lane = lax.broadcasted_iota(jnp.int32, (block, 128), 1)

    def body(step, _):
        here = pl.ds(pl.multiple_of(step * block, block), block)
        pos = step * block + lax.broadcasted_iota(jnp.int32, (block, width), 0)
        inside = (bounds[0:1, :] <= pos) & (bounds[1:2, :] > pos)
        mem = jnp.where(inside, 1.0, 0.0).astype(jnp.bfloat16)
        member[here, :] = mem
        rows_b = jnp.dot(mem, rows[...].reshape(width, 2 * HD), preferred_element_type=jnp.float32)
        picked[here, :] = rows_b.astype(jnp.bfloat16)
        score = jnp.sum(rows_b[:, HD:] * keys[here, :].astype(jnp.float32), axis=1, keepdims=True)
        e = jnp.exp(score * scale)
        pg = jnp.sum(rows_b[:, :HD] * values[here, :].astype(jnp.float32), axis=1, keepdims=True)
        expo[here, :] = e
        pgrad[here, :] = pg
        cols = jnp.zeros((block, 128), jnp.float32)
        for i, part in enumerate(split3(e) + split3(e * pg)):
            cols = jnp.where(lane == i, part, cols)
        cols_t = cols.T[:16].astype(jnp.bfloat16)
        sums[...] += jnp.dot(cols_t, mem, preferred_element_type=jnp.float32)
        return 0

    lax.fori_loop(first, last, body, 0)


def byte_table(sums, table):
    width = sums.shape[1]
    total = sums[0:1, :] + sums[1:2, :] + sums[2:3, :]
    inv = jnp.where(total > 0.0, 1.0 / jnp.where(total > 0.0, total, 1.0), 0.0)
    mass = (sums[3:4, :] + sums[4:5, :] + sums[5:6, :]) * inv
    row = lax.broadcasted_iota(jnp.int32, (128, width), 0)
    tab = jnp.zeros((128, width), jnp.float32)
    for i, part in enumerate(split3(inv) + split3(mass)):
        tab = jnp.where(row == i, part, tab)
    table[...] = tab.astype(jnp.bfloat16)


def byte_grads(block, scale, first, last, member, picked, expo, pgrad, table, gk, gv):
    lane = lax.broadcasted_iota(jnp.int32, (block, 128), 1)

    def body(step, _):
        here = pl.ds(pl.multiple_of(step * block, block), block)
        spread = lax.dot_general(
            member[here, :],
            table[...],
            (((1,), (1,)), ((), ())),
            preferred_element_type=jnp.float32,
        )
        inv = jnp.sum(jnp.where(lane < 3, spread, 0.0), axis=1, keepdims=True)
        mass = jnp.sum(jnp.where((lane >= 3) & (lane < 6), spread, 0.0), axis=1, keepdims=True)
        probs = expo[here, :] * inv
        sg = probs * (pgrad[here, :] - mass) * scale
        both = picked[here, :].astype(jnp.float32)
        gv[here, :] = (probs * both[:, :HD]).astype(jnp.bfloat16)
        gk[here, :] = (sg * both[:, HD:]).astype(jnp.bfloat16)
        return 0

    lax.fori_loop(first, last, body, 0)


def patch_kernel(
    ndp, nt, states, resid, up, gain, vw, ow, ctx, q, bounds, keys_in, values_in,
    wgv, wgo, gk_out, gv_out,
    wall, sqs, sqr, part, ws, yr, zs, zr, pas, par, gn, nrm, gpat, trans, gsend, grecv, qrecv,
    pay, keys, values, member, picked, expo, pgrad, sums, table, s_in, s_out,
    s_az, r_az, s_ay, r_ay, s_sq, r_sq, s_ry, r_ry, s_rz, r_rz, s_pa, r_pa, s_g, r_g,
):
    dp, sq, tn = lax.axis_index("dp"), lax.axis_index("seq"), lax.axis_index("tensor")
    patches, width = states.shape
    model = width * nt
    mine = dp * 2 + sq
    tall = 128
    nrow = patches // tall
    ncol = width // 256

    def zdev(k):
        return (lax.rem(dp + k, ndp), sq, tn)

    def tdev(k):
        return (dp, sq, lax.rem(tn + k, nt))

    ydev = (dp, 1 - sq, tn)

    def copy(src, dst, ssem, rsem, dev):
        return pltpu.make_async_remote_copy(
            src_ref=src, dst_ref=dst, send_sem=ssem, recv_sem=rsem,
            device_id=dev, device_id_type=pl.DeviceIdType.MESH,
        )

    k_in = pltpu.make_async_copy(keys_in, keys, s_in.at[0])
    v_in = pltpu.make_async_copy(values_in, values, s_in.at[1])
    k_in.start()
    v_in.start()

    barrier = pltpu.get_barrier_semaphore()
    peers = [zdev(k) for k in range(1, ndp)] + [tdev(k) for k in range(1, nt)] + [ydev]
    for dev in peers:
        pl.semaphore_signal(barrier, inc=1, device_id=dev, device_id_type=pl.DeviceIdType.MESH)
    pl.semaphore_wait(barrier, len(peers))

    sent = []

    def go(c):
        c.start()
        sent.append(c)
        return c

    weights = (vw, ow)

    def gather_start(w):
        z = [
            go(copy(weights[w], wall.at[w, mine], s_az.at[w, k - 1], r_az.at[w, k - 1], zdev(k)))
            for k in range(1, ndp)
        ]
        y = [go(copy(weights[w], wall.at[w, mine], s_ay.at[w, 0], r_ay.at[w, 0], ydev))]
        return z, y

    def gather_forward(w, z, y):
        for k in range(1, ndp):
            z[k - 1].wait_recv()
            slot = lax.rem(dp + (ndp - k), ndp) * 2 + sq
            y.append(
                go(copy(wall.at[w, slot], wall.at[w, slot], s_ay.at[w, k], r_ay.at[w, k], ydev))
            )

    vz, vy = gather_start(0)
    qc = go(copy(q, qrecv, s_g.at[0], r_g.at[0], ydev))

    def row_loop(fn):
        def body(i, _):
            fn(pl.ds(pl.multiple_of(i * tall, tall), tall), i)
            return 0

        lax.fori_loop(0, nrow, body, 0)

    def to_row(col):
        return jnp.broadcast_to(col, (tall, 128)).T[:8]

    def total_of(which):
        rows = sqs[which] + sqr[which, 0]
        for k in range(1, nt - 1):
            rows = rows + sqr[which, k]
        return rows

    def share(which):
        return [
            go(copy(sqs.at[which], sqr.at[which, k - 1], s_sq.at[which, k - 1],
                    r_sq.at[which, k - 1], tdev(k)))
            for k in range(1, nt)
        ]

    def column(rows):
        return jnp.broadcast_to(rows[0:1, :], (128, patches)).T

    def square(here, i):
        x = states[here, :].astype(jnp.float32)
        sqs[0, i] = to_row(jnp.sum(x * x, axis=1, keepdims=True))

    row_loop(square)
    sq_copies = share(0)
    oz, oy = gather_start(1)
    wall[0, mine] = vw[...]
    wall[1, mine] = ow[...]
    gather_forward(0, vz, vy)
    for c in sq_copies:
        c.wait_recv()

    def inverse(i):
        rows = sqs[0, i]
        for k in range(nt - 1):
            rows = rows + sqr[0, k, i]
        col = jnp.broadcast_to(rows[0:1, :], (128, tall)).T[:, 0:1]
        return lax.rsqrt(col / model + 1e-05)

    def normalise(here, i):
        x = states[here, :].astype(jnp.float32)
        nrm[here, :] = (x * inverse(i) * gain[...].astype(jnp.float32)).astype(jnp.bfloat16)

    row_loop(normalise)

    def wgrad(w, left, right):
        trans[...] = left[...].T
        nblk, rows_per = part.shape[1], part.shape[2]

        def body(c, _):
            cols = pl.ds(pl.multiple_of(c * 256, 256), 256)
            out = jnp.dot(trans[...], right[:, cols], preferred_element_type=jnp.float32)
            part[w, :, :, cols] = out.reshape(nblk, rows_per, 256)
            return 0

        lax.fori_loop(0, ncol, body, 0)
        copies = []
        for j in range(ndp):
            ws[w, j] = part[w, j * 2 + (1 - sq)].astype(jnp.bfloat16)
            copies.append(go(copy(ws.at[w, j], yr.at[w, j], s_ry.at[w, j], r_ry.at[w, j], ydev)))
        return copies

    def wgrad_forward(w, copies):
        for c in copies:
            c.wait_recv()
        out = []
        for k in range(1, ndp):
            t = lax.rem(dp + k, ndp)
            zs[w, k - 1] = (part[w, t * 2 + sq] + yr[w, t].astype(jnp.float32)).astype(jnp.bfloat16)
            out.append(
                go(copy(zs.at[w, k - 1], zr.at[w, k - 1], s_rz.at[w, k - 1], r_rz.at[w, k - 1],
                        zdev(k)))
            )
        return out

    def wgrad_finish(w, copies, dst):
        total = part[w, mine] + yr[w, dp].astype(jnp.float32)
        for k, c in enumerate(copies):
            c.wait_recv()
            total = total + zr[w, k].astype(jnp.float32)
        dst[...] = total

    for c in vy:
        c.wait_recv()

    def project(here, i):
        full = wall[0].reshape(up.shape[1], width)
        g = jnp.dot(up[here, :], full, preferred_element_type=jnp.float32)
        gn[here, :] = g
        x = states[here, :].astype(jnp.float32)
        cross = g * gain[...].astype(jnp.float32) * x
        sqs[1, i] = to_row(jnp.sum(cross, axis=1, keepdims=True))

    row_loop(project)
    cr_copies = share(1)
    gather_forward(1, oz, oy)
    for c in cr_copies:
        c.wait_recv()

    def make_grad(here, i):
        inv = inverse(i)
        rows = sqs[1, i]
        for k in range(nt - 1):
            rows = rows + sqr[1, k, i]
        cross = jnp.broadcast_to(rows[0:1, :], (128, tall)).T[:, 0:1] / model
        x = states[here, :].astype(jnp.float32)
        gpat[here, :] = (
            resid[here, :].astype(jnp.float32)
            + inv * gain[...].astype(jnp.float32) * gn[here, :]
            - (inv * inv * inv * cross) * x
        ).astype(jnp.bfloat16)

    row_loop(make_grad)
    for c in oy:
        c.wait_recv()

    def attn(here, i):
        full = wall[1].reshape(up.shape[1], width)
        p = lax.dot_general(
            gpat[here, :], full, (((1,), (1,)), ((), ())), preferred_element_type=jnp.float32
        )
        for j in range(nt):
            pas[j, here, :] = p[:, j * HD : (j + 1) * HD]

    row_loop(attn)
    for k in range(1, nt):
        ws_slot = lax.rem(tn + k, nt)
        gsend[k] = pas[ws_slot].astype(jnp.bfloat16)
    pa_copies = [
        go(copy(gsend.at[k], par.at[k - 1], s_pa.at[k - 1], r_pa.at[k - 1], tdev(k)))
        for k in range(1, nt)
    ]
    wv_y = wgrad(0, up, nrm)
    total = pas[tn]
    for k, c in enumerate(pa_copies):
        c.wait_recv()
        total = total + par[k].astype(jnp.float32)
    gsend[0] = total.astype(jnp.bfloat16)
    gc = go(copy(gsend.at[0], grecv, s_g.at[1], r_g.at[1], ydev))
    wo_y = wgrad(1, ctx, gpat)
    sums[...] = jnp.zeros_like(sums)
    pay[sq, :, :HD] = gsend[0]
    pay[sq, :, HD:] = q[...]
    k_in.wait()
    v_in.wait()
    qc.wait_recv()
    gc.wait_recv()
    pay[1 - sq, :, :HD] = grecv[...]
    pay[1 - sq, :, HD:] = qrecv[...]
    block = 512
    steps = keys.shape[0] // block
    scale = 1.0 / math.sqrt(HD)
    args = (bounds, pay, keys, values, member, picked, expo, pgrad, sums)
    byte_sums(block, scale, 0, steps // 4, *args)
    wv_z = wgrad_forward(0, wv_y)
    byte_sums(block, scale, steps // 4, 3 * steps // 4, *args)
    wo_z = wgrad_forward(1, wo_y)
    byte_sums(block, scale, 3 * steps // 4, steps, *args)
    byte_table(sums, table)
    byte_grads(block, scale, 0, steps, member, picked, expo, pgrad, table, keys, values)
    k_out = pltpu.make_async_copy(keys, gk_out, s_out.at[0])
    v_out = pltpu.make_async_copy(values, gv_out, s_out.at[1])
    k_out.start()
    v_out.start()
    wgrad_finish(0, wv_z, wgv)
    wgrad_finish(1, wo_z, wgo)
    k_out.wait()
    v_out.wait()
    for c in sent:
        c.wait_send()


def patch_backward(ndp, nt, states, resid, up, gain, vw, ow, ctx, q, bounds, keys, values):
    patches, width = states.shape
    rows = vw.shape[0]
    nblk = 2 * ndp
    nbytes = keys.shape[0]
    bf, f32 = jnp.bfloat16, jnp.float32
    nrow = patches // 128
    vmem = pl.BlockSpec(memory_space=pltpu.VMEM)
    dma = pltpu.SemaphoreType.DMA
    return pl.pallas_call(
        functools.partial(patch_kernel, ndp, nt),
        out_shape=(
            jax.ShapeDtypeStruct((rows, width), f32),
            jax.ShapeDtypeStruct((rows, width), f32),
            jax.ShapeDtypeStruct(keys.shape, bf),
            jax.ShapeDtypeStruct(keys.shape, bf),
        ),
        in_specs=[vmem] * 9 + [pl.BlockSpec(memory_space=pl.ANY)] * 2,
        out_specs=[vmem] * 2 + [pl.BlockSpec(memory_space=pl.ANY)] * 2,
        scratch_shapes=[
            pltpu.VMEM((2, nblk, rows, width), bf),
            pltpu.VMEM((2, nrow, 8, 128), f32),
            pltpu.VMEM((2, nt - 1, nrow, 8, 128), f32),
            pltpu.VMEM((2, nblk, rows, width), f32),
            pltpu.VMEM((2, ndp, rows, width), bf),
            pltpu.VMEM((2, ndp, rows, width), bf),
            pltpu.VMEM((2, ndp - 1, rows, width), bf),
            pltpu.VMEM((2, ndp - 1, rows, width), bf),
            pltpu.VMEM((nt, patches, HD), f32),
            pltpu.VMEM((nt - 1, patches, HD), bf),
            pltpu.VMEM((patches, width), f32),
            pltpu.VMEM((patches, width), bf),
            pltpu.VMEM((patches, width), bf),
            pltpu.VMEM((nblk * rows, patches), bf),
            pltpu.VMEM((nt, patches, HD), bf),
            pltpu.VMEM((patches, HD), bf),
            pltpu.VMEM((patches, HD), bf),
            pltpu.VMEM((2, patches, 2 * HD), bf),
            pltpu.VMEM(keys.shape, bf),
            pltpu.VMEM(keys.shape, bf),
            pltpu.VMEM((nbytes, 2 * patches), bf),
            pltpu.VMEM((nbytes, 2 * HD), bf),
            pltpu.VMEM((nbytes, 1), f32),
            pltpu.VMEM((nbytes, 1), f32),
            pltpu.VMEM((16, 2 * patches), f32),
            pltpu.VMEM((128, 2 * patches), bf),
            dma((2,)), dma((2,)),
            dma((2, ndp - 1)), dma((2, ndp - 1)),
            dma((2, ndp)), dma((2, ndp)),
            dma((2, nt - 1)), dma((2, nt - 1)),
            dma((2, ndp)), dma((2, ndp)),
            dma((2, ndp - 1)), dma((2, ndp - 1)),
            dma((nt - 1,)), dma((nt - 1,)),
            dma((2,)), dma((2,)),
        ],
        compiler_params=pltpu.CompilerParams(
            collective_id=0, has_side_effects=True, vmem_limit_bytes=62 * 1024 * 1024
        ),
    )(states, resid, up, gain, vw, ow, ctx, q, bounds, keys, values)


def on_device_kernels(
    ndp, nt, patch_states, residual_grad, upstream_value, norm_gain, value_weight, out_weight,
    attn_out, queries, byte_keys, byte_values, patch_starts,
):
    byte_count = byte_keys.shape[1]
    starts = patch_starts[0] - lax.axis_index("seq") * byte_count
    after = jnp.concatenate([starts[1:], jnp.full((1,), 2 * byte_count, jnp.int32)])
    wgv, wgo, gk, gv = patch_backward(
        ndp, nt, patch_states[0], residual_grad[0], upstream_value[0], norm_gain[None],
        value_weight, out_weight, attn_out[0], queries[0],
        jnp.stack([starts, after]), byte_keys[0], byte_values[0],
    )
    return (wgv, wgo, gk[None], gv[None])


def solution(mesh):
    ndp, nseq, nt = mesh.shape["dp"], mesh.shape["seq"], mesh.shape["tensor"]
    use_kernels = nseq == 2 and ndp <= 4
    body = functools.partial(on_device_kernels, ndp, nt) if use_kernels else on_device
    return jax.shard_map(
        body,
        mesh=mesh,
        in_specs=(
            P("dp", "seq", "tensor"),
            P("dp", "seq", "tensor"),
            P("dp", "seq", None),
            P("tensor"),
            P(("dp", "seq"), "tensor"),
            P(("dp", "seq"), "tensor"),
            P("dp", "seq", None),
            P("dp", "seq", "tensor"),
            P("dp", "seq", "tensor"),
            P("dp", "seq", "tensor"),
            P("dp", None),
        ),
        out_specs=(
            P(("dp", "seq"), "tensor"),
            P(("dp", "seq"), "tensor"),
            P("dp", "seq", "tensor"),
            P("dp", "seq", "tensor"),
        ),
        check_vma=False,
    )
```

profile of v0, /device:TPU:0, one launch (start us, length us, event | category | flops | bytes accessed | tf_op | source)
XLA Modules:
  0.0 100.5 jit_solution(17036646514320492242)
XLA Ops:
  0.6 0.7 broadcast_subtract_fusion
  1.3 0.1 slice_reduce_fusion
  1.4 0.1 pad_add_fusion.1
  1.5 0.6 pad_add_fusion.bounds
  2.1 1.3 %broadcast_in_dim.9.gain = bf16[1,1024]{1,0:T(2,128)(2,1)} reshape(bf16[1024]{0:T(1024)(128)(2,1)} %param.14) | data formatting | bytes 4096 | tf_op jit(solution)/shard_map/broadcast_in_dim | solution.py:544
  3.4 89.2 %shard_map.138 = (f32[64,1024]{1,0:T(8,128)}, f32[64,1024]{1,0:T(8,128)}, bf16[8192,128]{1,0:T(8,128)(2,1)}, bf16[8192,128]{1,0:T(8,128)(2,1)}) custom-call(bf16[384,1024]{1,0:T(8,128)(2,1)} %bitcast.13, bf16[384,1024]{1,0:T(8,128)(2,1)} %bitcast.14, bf16[384,512]{1,0:T(8,128)(2,1)} %bitcast.15, bf16[1,1024]{1,0:T(2,128)(2,1)} %broadcast_in_dim.9.gain, ...), custom_call_target="tpu_custom_call" | custom-call | tf_op jit(solution)/shard_map/pallas_call | solution.py:484
  92.6 1.7 %copy.19 = f32[64,1024]{1,0:T(8,128)} copy(f32[64,1024]{1,0:T(8,128)} %get-tuple-element.16) | data formatting | bytes 524288
  94.3 1.7 %copy.20 = f32[64,1024]{1,0:T(8,128)} copy(f32[64,1024]{1,0:T(8,128)} %get-tuple-element.17) | data formatting | bytes 524288
  96.0 0.0 copy-start
  96.0 3.2 %copy.21 = bf16[1,8192,128]{2,1,0:T(8,128)(2,1)} copy(bf16[1,8192,128]{2,1,0:T(8,128)(2,1)} %bitcast.12) | data formatting | bytes 4194304
  99.1 0.0 copy-done
  99.2 1.3 %copy.22 = bf16[1,8192,128]{2,1,0:T(8,128)(2,1)} copy(bf16[1,8192,128]{2,1,0:T(8,128)(2,1)S(1)} %bitcast.11) | data formatting | bytes 4194304
  (1 shorter events, 0.0 us)
Async XLA Ops:
  96.0 3.2 %copy-start = (bf16[8192,128]{1,0:T(8,128)(2,1)S(1)}, bf16[8192,128]{1,0:T(8,128)(2,1)}, u32[]{:S(2)}) copy-start(bf16[8192,128]{1,0:T(8,128)(2,1)} %get-tuple-element.11) | copy-start | bytes 6291460
where the time goes:
time: 102 us; the launch traced here: 100 us
  Pallas kernels  89.2 us (87%)
  local copies, waits for them, and re-layouts  9.23 us (9%)
  other arithmetic  1.37 us (1%)
    pallas_call x1, Pallas kernels, patch_backward(): pl.pallas_call(functools.partial(patch_kernel, ndp, nt), out_shape=(jax.S...  89.2 us
    unnamed x6, local copies, waits for them, and re-layouts  7.86 us

commit v1 on v0

v1 whole, which is shorter than its diff:
```python
import functools
import math

import jax
import jax.numpy as jnp
from jax import lax
from jax.experimental import pallas as pl
from jax.experimental.pallas import tpu as pltpu
from jax.sharding import PartitionSpec as P

HD = 128


def member_sum(member32, terms):
    return lax.dot_general(
        member32,
        terms,
        (((0,), (0,)), ((), ())),
        precision=lax.Precision.HIGHEST,
        preferred_element_type=jnp.float32,
    )


def member_spread(member32, totals):
    return jnp.dot(
        member32, totals, precision=lax.Precision.HIGHEST, preferred_element_type=jnp.float32
    )


def cross_backward(member, segment_rows, keys, values, head_width):
    nbytes = keys.shape[0]
    heads = keys.shape[1] // HD
    scale = 1.0 / math.sqrt(HD)
    member32 = member.astype(jnp.float32)
    picked = jnp.dot(member, segment_rows, preferred_element_type=jnp.float32).astype(jnp.bfloat16)
    grad_f = picked[:, :head_width].astype(jnp.float32).reshape(nbytes, heads, HD)
    query_f = picked[:, head_width:].astype(jnp.float32).reshape(nbytes, heads, HD)
    keys_f = keys.astype(jnp.float32).reshape(nbytes, heads, HD)
    values_f = values.astype(jnp.float32).reshape(nbytes, heads, HD)
    scores = jnp.sum(query_f * keys_f, axis=-1) * scale
    expo = jnp.exp(scores)
    totals = member_spread(member32, member_sum(member32, expo))
    probs = expo / totals
    grad_values = (probs[..., None] * grad_f).reshape(nbytes, heads * HD).astype(jnp.bfloat16)
    prob_grad = jnp.sum(grad_f * values_f, axis=-1)
    mass = member_spread(member32, member_sum(member32, probs * prob_grad))
    score_grad = probs * (prob_grad - mass)
    grad_keys = (
        (score_grad[..., None] * query_f * scale).reshape(nbytes, heads * HD).astype(jnp.bfloat16)
    )
    return (grad_keys, grad_values)


def contract_rows(left, right):
    return lax.dot_general(
        left, right, (((0,), (0,)), ((), ())), preferred_element_type=jnp.float32
    )


def on_device(
    patch_states,
    residual_grad,
    upstream_value,
    norm_gain,
    value_weight,
    out_weight,
    attn_out,
    queries,
    byte_keys,
    byte_values,
    patch_starts,
):
    states = patch_states[0]
    patches = states.shape[0]
    width_local = states.shape[1]
    model_width = width_local * lax.axis_size("tensor")
    states32 = states.astype(jnp.float32)
    gain32 = norm_gain.astype(jnp.float32)
    upstream = upstream_value[0]
    context = attn_out[0]
    value_full, out_full = (
        lax.all_gather(value_weight, ("dp", "seq"), axis=0, tiled=True),
        lax.all_gather(out_weight, ("dp", "seq"), axis=0, tiled=True),
    )
    grad_normed = jnp.dot(upstream, value_full, preferred_element_type=jnp.float32)
    square_part = jnp.sum(states32 * states32, axis=1)
    cross_part = jnp.sum(grad_normed * gain32 * states32, axis=1)
    square_sum, cross_sum = lax.psum((square_part, cross_part), "tensor")
    inv_rms = lax.rsqrt(square_sum / model_width + 1e-05)
    normed = (states32 * inv_rms[:, None] * gain32).astype(jnp.bfloat16)
    grad_patch = (
        residual_grad[0].astype(jnp.float32)
        + inv_rms[:, None] * gain32 * grad_normed
        - (inv_rms**3)[:, None] * states32 * (cross_sum / model_width)[:, None]
    ).astype(jnp.bfloat16)
    partial_attn = lax.dot_general(
        grad_patch, out_full, (((1,), (1,)), ((), ())), preferred_element_type=jnp.float32
    )
    columns = upstream
    wgrad_value = lax.psum_scatter(
        contract_rows(columns, normed), ("dp", "seq"), scatter_dimension=0, tiled=True
    )
    columns = context
    wgrad_out = lax.psum_scatter(
        contract_rows(columns, grad_patch), ("dp", "seq"), scatter_dimension=0, tiled=True
    )
    attn_all = lax.psum(partial_attn, "tensor").astype(jnp.bfloat16)
    head_width = queries.shape[2]
    grad_attn = lax.dynamic_slice_in_dim(
        attn_all, lax.axis_index("tensor") * head_width, head_width, 1
    )
    starts = patch_starts[0]
    total_patches = starts.shape[0]
    seq_count = lax.axis_size("seq")
    seq_pos = lax.axis_index("seq")
    byte_count = byte_keys.shape[1]
    window_len = 2 * patches
    owners = starts // byte_count
    shard_ids = jnp.arange(seq_count, dtype=jnp.int32)
    firsts = jnp.sum((owners[None, :] < shard_ids[:, None]).astype(jnp.int32), axis=1)
    my_first = jnp.sum(firsts * (shard_ids == seq_pos).astype(jnp.int32))
    payload = jnp.concatenate([grad_attn, queries[0]], axis=1)
    padded_starts = jnp.concatenate(
        [starts, jnp.full((window_len,), 2 * total_patches * byte_count + byte_count, jnp.int32)]
    )
    local_starts = lax.dynamic_slice_in_dim(padded_starts, my_first, window_len)
    positions = seq_pos * byte_count + jnp.arange(byte_count, dtype=jnp.int32)
    reached = local_starts[None, :] <= positions[:, None]
    after = jnp.concatenate([reached[:, 1:], jnp.zeros((byte_count, 1), bool)], axis=1)
    member = (reached & jnp.logical_not(after)).astype(jnp.bfloat16)
    mine = seq_pos * patches + jnp.arange(patches, dtype=jnp.int32)
    targets = lax.dynamic_slice_in_dim(owners, seq_pos * patches, patches)
    target_first = jnp.sum((owners[None, :] < targets[:, None]).astype(jnp.int32), axis=1)
    slots = mine - jnp.maximum(seq_pos * patches, target_first)
    dest = targets * patches + slots
    place = (jnp.arange(seq_count * patches, dtype=jnp.int32)[:, None] == dest[None, :]).astype(
        jnp.bfloat16
    )
    outgoing = jnp.dot(place, payload, preferred_element_type=jnp.float32).astype(jnp.bfloat16)
    outgoing = outgoing.reshape(seq_count, patches, 2 * head_width)
    incoming = lax.all_to_all(outgoing, "seq", split_axis=0, concat_axis=0, tiled=True)
    wanted = my_first + jnp.arange(window_len, dtype=jnp.int32)
    sources = wanted // patches
    received_row = sources * patches + wanted - jnp.maximum(sources * patches, my_first)
    select = (
        received_row[:, None] == jnp.arange(seq_count * patches, dtype=jnp.int32)[None, :]
    ).astype(jnp.bfloat16)
    segment_rows = jnp.dot(
        select,
        incoming.reshape(seq_count * patches, 2 * head_width),
        preferred_element_type=jnp.float32,
    ).astype(jnp.bfloat16)
    grad_keys, grad_values = cross_backward(
        member, segment_rows, byte_keys[0], byte_values[0], head_width
    )
    return (wgrad_value, wgrad_out, grad_keys[None], grad_values[None])


BLK = 256
WIN = 128


def grad_kernel(
    ndp, nt, nbytes, states_in, resid_in, up_in, gain_in, vw, ow, ctx_in, q_in, starts,
    wgv, wgo, g_out, q_out, tab, bounds,
    states, resid, up, ctx, gain, wall, sqs, sqr, part, acc, rbv, lbv, ysv, yrv, rbo, lbo, yso, yro,
    pas, par, gn, nrm, gpat, trans_v, trans_o, gsend, gboth, qboth,
    s_in, s_own, s_out, s_ag, r_ag, s_sq, r_sq, s_rv, r_rv, s_lv, r_lv, s_ro, r_ro, s_lo, r_lo,
    s_yo, r_yo, s_yv, r_yv, s_pa, r_pa, s_g, r_g,
):
    dp, sq, tn = lax.axis_index("dp"), lax.axis_index("seq"), lax.axis_index("tensor")
    patches, width = states.shape
    model = width * nt
    last = ndp - 1
    mine = dp * 2 + sq
    tall = 128
    nrow = patches // tall
    ncol = width // 256

    right, left = (dp + 1, sq, tn), (dp - 1, sq, tn)
    ydev = (dp, 1 - sq, tn)

    def tdev(k):
        return (dp, sq, lax.rem(tn + k, nt))

    def copy(src, dst, ssem, rsem, dev):
        return pltpu.make_async_remote_copy(
            src_ref=src, dst_ref=dst, send_sem=ssem, recv_sem=rsem,
            device_id=dev, device_id_type=pl.DeviceIdType.MESH,
        )

    local = {}
    for i, (name, src, dst) in enumerate(
        (("states", states_in, states), ("up", up_in, up), ("resid", resid_in, resid),
         ("ctx", ctx_in, ctx), ("q", q_in, qboth.at[sq]), ("vw", vw, wall.at[0, mine]),
         ("ow", ow, wall.at[1, mine]))
    ):
        local[name] = pltpu.make_async_copy(src, dst, s_in.at[i])
        local[name].start()

    barrier = pltpu.get_barrier_semaphore()
    peers = [(lax.rem(dp + k, ndp), sq, tn) for k in range(1, ndp)]
    peers += [tdev(k) for k in range(1, nt)] + [ydev]
    for dev in peers:
        pl.semaphore_signal(barrier, inc=1, device_id=dev, device_id_type=pl.DeviceIdType.MESH)
    pl.semaphore_wait(barrier, len(peers))

    sent = []

    def go(c, cond=None):
        if cond is None:
            c.start()
        else:
            pl.when(cond)(c.start)
        sent.append((c, cond))
        return c

    weights = (vw, ow)

    def shard(w, zz, yy, dev, k, own=False):
        slot = zz * 2 + yy
        src = weights[w] if own else wall.at[w, slot]
        return copy(src, wall.at[w, slot], s_ag.at[w, k], r_ag.at[w, slot], dev)

    def ag_own_z(w):
        go(shard(w, dp, sq, right, 0, True), dp < last)
        go(shard(w, dp, sq, left, 1, True), dp > 0)

    def ag_own_y(w):
        go(shard(w, dp, sq, ydev, 2, True))

    def ag_forward(w, s):
        for zz, here, dev, onward, k in (
            (dp - s, dp - s >= 0, right, dp < last, 3 * s),
            (dp + s, dp + s <= last, left, dp > 0, 3 * ndp + 3 * s),
        ):
            pl.when(here)(shard(w, zz, sq, dev, k).wait_recv)
            go(shard(w, zz, sq, dev, k), here & onward)
            go(shard(w, zz, sq, ydev, k + 1), here)

    def ag_wait_y(w):
        for zz in range(ndp):
            shard(w, zz, 1 - sq, ydev, 2).wait_recv()

    def row_loop(fn):
        def body(i, _):
            fn(pl.ds(pl.multiple_of(i * tall, tall), tall), i)
            return 0

        lax.fori_loop(0, nrow, body, 0)

    def to_row(col):
        return jnp.broadcast_to(col, (tall, 128)).T[:8]

    def share(which):
        return [
            go(copy(sqs.at[which], sqr.at[which, k - 1], s_sq.at[which, k - 1],
                    r_sq.at[which, k - 1], tdev(k)))
            for k in range(1, nt)
        ]

    def total_col(which, i):
        rows = sqs[which, i]
        for k in range(nt - 1):
            rows = rows + sqr[which, k, i]
        return jnp.broadcast_to(rows[0:1, :], (128, tall)).T[:, 0:1]

    def inverse(i):
        return lax.rsqrt(total_col(0, i) / model + 1e-05)

    def square(here, i):
        x = states[here, :].astype(jnp.float32)
        sqs[0, i] = to_row(jnp.sum(x * x, axis=1, keepdims=True))

    def normalise(here, i):
        x = states[here, :].astype(jnp.float32)
        nrm[here, :] = (x * inverse(i) * gain[0:1, :]).astype(jnp.bfloat16)

    def wgrad(w, trans, factor):
        nblk, rows_per = part.shape[1], part.shape[2]

        def body(c, _):
            cols = pl.ds(pl.multiple_of(c * 256, 256), 256)
            out = jnp.dot(trans[...], factor[:, cols], preferred_element_type=jnp.float32)
            part[w, :, :, cols] = out.reshape(nblk, rows_per, 256)
            return 0

        lax.fori_loop(0, ncol, body, 0)

    def two(zz):
        return part[0, pl.ds(zz * 2, 2)]

    def one(zz):
        yo(zz).wait_recv()
        return part[1, zz * 2 + sq] + yro[zz].astype(jnp.float32)

    def line(d, get, buf_r, buf_l, s_r, r_r, s_l, r_l):
        for zz, valid, dev, fed, buf, ss, rs in (
            (dp + d, dp + d <= last, right, dp > 0, buf_r, s_r, r_r),
            (dp - d, dp - d >= 0, left, dp < last, buf_l, s_l, r_l),
        ):
            c = copy(buf.at[zz], buf.at[zz], ss.at[d - 1], rs.at[zz], dev)

            @pl.when(valid)
            def _(zz=zz, fed=fed, buf=buf, c=c):
                mine_part = get(zz)

                @pl.when(fed)
                def _():
                    c.wait_recv()
                    buf[zz] = (mine_part + buf[zz].astype(jnp.float32)).astype(jnp.bfloat16)

                @pl.when(jnp.logical_not(fed))
                def _():
                    buf[zz] = mine_part.astype(jnp.bfloat16)

            go(c, valid)

    def line_end(rows, buf_r, buf_l, s_r, r_r, s_l, r_l):
        for fed, dev, buf, ss, rs in (
            (dp > 0, right, buf_r, s_r, r_r),
            (dp < last, left, buf_l, s_l, r_l),
        ):
            c = copy(buf.at[dp], buf.at[dp], ss.at[0], rs.at[dp], dev)

            @pl.when(fed)
            def _(c=c, buf=buf):
                c.wait_recv()
                acc[rows] += buf[dp].astype(jnp.float32)

    line_v = (rbv, lbv, s_rv, r_rv, s_lv, r_lv)
    line_o = (rbo, lbo, s_ro, r_ro, s_lo, r_lo)

    def yo(zz):
        return copy(yso.at[zz], yro.at[zz], s_yo.at[zz], r_yo.at[zz], ydev)

    def send_yo(zz, cond=None):
        def fill():
            yso[zz] = part[1, zz * 2 + (1 - sq)].astype(jnp.bfloat16)

        fill() if cond is None else pl.when(cond)(fill)
        go(yo(zz), cond)

    ag_own_z(0)
    ag_own_y(0)
    for i in range(width // 128):
        gain[:, i * 128 : (i + 1) * 128] = jnp.broadcast_to(
            gain_in[i : i + 1, :].astype(jnp.float32), (8, 128)
        )
    local["states"].wait()
    row_loop(square)
    sq_copies = share(0)
    local["up"].wait()
    trans_v[...] = up[...].T

    first = starts[0:1, :] - sq * nbytes
    row8 = jnp.broadcast_to(first, (8, first.shape[1]))
    lane = lax.broadcasted_iota(jnp.int32, row8.shape, 1)
    after = jnp.where(
        lane == first.shape[1] - 1, 2 * nbytes, pltpu.roll(row8, first.shape[1] - 1, 1)
    )
    far = jnp.full((1, WIN), 4 * nbytes, jnp.int32)
    bounds[0:1, : first.shape[1]] = first
    bounds[1:2, : first.shape[1]] = after[0:1, :]
    bounds[0:1, first.shape[1] :] = far
    bounds[1:2, first.shape[1] :] = far

    ag_forward(0, 1)
    for c in sq_copies:
        c.wait_recv()
    row_loop(normalise)
    wgrad(0, trans_v, nrm)
    line(3, two, *line_v)

    nblocks = nbytes // BLK
    ends = lax.broadcasted_iota(jnp.int32, (nblocks, first.shape[1]), 0) * BLK + (BLK - 1)
    reach = (jnp.broadcast_to(first, ends.shape) <= ends).astype(jnp.int32)
    high = (jnp.sum(reach, axis=1, keepdims=True) - 1) // WIN
    low = (jnp.sum((first <= 0).astype(jnp.int32), axis=1, keepdims=True) - 1) // WIN
    step = lax.broadcasted_iota(jnp.int32, (nblocks, 128), 0) + high - low
    pair = lax.broadcasted_iota(jnp.int32, (nblocks, 128), 1)
    block_of = jnp.sum((step < pair).astype(jnp.int32), axis=0, keepdims=True)
    window = lax.broadcasted_iota(jnp.int32, (1, 128), 1) - block_of + low
    done = block_of >= nblocks
    tab[0:1, :] = jnp.where(done, nblocks - 1, block_of)
    tab[1:2, :] = jnp.where(done, first.shape[1] // WIN, window)

    ag_forward(0, 2)
    ag_own_z(1)
    ag_forward(0, 3)
    ag_own_y(1)
    local["ctx"].wait()
    trans_o[...] = ctx[...].T
    line(2, two, *line_v)
    ag_forward(1, 1)
    local["vw"].wait()
    ag_wait_y(0)

    def project(here, i):
        full = wall[0].reshape(up.shape[1], width)
        g = jnp.dot(up[here, :], full, preferred_element_type=jnp.float32)
        gn[here, :] = g
        x = states[here, :].astype(jnp.float32)
        sqs[1, i] = to_row(jnp.sum(g * gain[0:1, :] * x, axis=1, keepdims=True))

    row_loop(project)
    cr_copies = share(1)
    ag_forward(1, 2)
    line(1, two, *line_v)
    local["resid"].wait()
    for c in cr_copies:
        c.wait_recv()

    def make_grad(here, i):
        inv = inverse(i)
        cross = total_col(1, i) / model
        x = states[here, :].astype(jnp.float32)
        gpat[here, :] = (
            resid[here, :].astype(jnp.float32)
            + inv * gain[0:1, :] * gn[here, :]
            - (inv * inv * inv * cross) * x
        ).astype(jnp.bfloat16)

    row_loop(make_grad)
    ag_forward(1, 3)
    wgrad(1, trans_o, gpat)
    local["q"].wait()
    qc = go(copy(qboth.at[sq], qboth.at[sq], s_g.at[0], r_g.at[0], ydev))
    for k in range(ndp - 1, 0, -1):
        send_yo(dp + k, dp + k <= last)
        send_yo(dp - k, dp - k >= 0)
    send_yo(dp)
    local["ow"].wait()
    ag_wait_y(1)

    def attn(here, i):
        full = wall[1].reshape(up.shape[1], width)
        p = lax.dot_general(
            gpat[here, :], full, (((1,), (1,)), ((), ())), preferred_element_type=jnp.float32
        )
        for j in range(nt):
            pas[j, here, :] = p[:, j * HD : (j + 1) * HD]

    row_loop(attn)
    pa_copies = []
    for k in range(1, nt):
        gsend[k - 1] = pas[lax.rem(tn + k, nt)].astype(jnp.bfloat16)
        pa_copies.append(
            go(copy(gsend.at[k - 1], par.at[k - 1], s_pa.at[k - 1], r_pa.at[k - 1], tdev(k)))
        )

    acc[...] = two(dp)
    line_end(pl.ds(0, 2), *line_v)
    ysv[...] = acc[1 - sq].astype(jnp.bfloat16)
    yv = go(copy(ysv, yrv, s_yv.at[0], r_yv.at[0], ydev))

    total = pas[tn]
    for k, c in enumerate(pa_copies):
        c.wait_recv()
        total = total + par[k].astype(jnp.float32)
    gboth[sq] = total.astype(jnp.bfloat16)
    gc = go(copy(gboth.at[sq], gboth.at[sq], s_g.at[1], r_g.at[1], ydev))

    line(3, one, *line_o)
    line(2, one, *line_o)
    yv.wait_recv()
    acc[0] = acc[sq] + yrv[...].astype(jnp.float32)
    out_v = pltpu.make_async_copy(acc.at[0], wgv, s_out.at[0])
    out_v.start()
    line(1, one, *line_o)
    acc[1] = one(dp)
    line_end(1, *line_o)
    out_o = pltpu.make_async_copy(acc.at[1], wgo, s_out.at[1])
    out_o.start()
    qc.wait_recv()
    gc.wait_recv()
    out_q = pltpu.make_async_copy(qboth, q_out, s_out.at[2])
    out_q.start()
    out_g = pltpu.make_async_copy(gboth, g_out, s_out.at[3])
    out_g.start()
    for c, cond in sent:
        if cond is None:
            c.wait_send()
        else:
            pl.when(cond)(c.wait_send)
    for c in (out_v, out_o, out_q, out_g):
        c.wait()


def grad_call(ndp, nt, nbytes, states, resid, up, gain, vw, ow, ctx, q, starts):
    patches, width = states.shape
    rows = vw.shape[0]
    nblk = 2 * ndp
    nk = up.shape[1]
    bf, f32, i32 = jnp.bfloat16, jnp.float32, jnp.int32
    nrow = patches // 128
    total = starts.shape[1]
    vmem = pl.BlockSpec(memory_space=pltpu.VMEM)
    hbm = pl.BlockSpec(memory_space=pl.ANY)
    dma = pltpu.SemaphoreType.DMA
    return pl.pallas_call(
        functools.partial(grad_kernel, ndp, nt, nbytes),
        out_shape=(
            jax.ShapeDtypeStruct((rows, width), f32),
            jax.ShapeDtypeStruct((rows, width), f32),
            jax.ShapeDtypeStruct((2, patches, HD), bf),
            jax.ShapeDtypeStruct((2, patches, HD), bf),
            jax.ShapeDtypeStruct((2, 128), i32),
            jax.ShapeDtypeStruct((2, total + WIN), i32),
        ),
        in_specs=[hbm, hbm, hbm, vmem, hbm, hbm, hbm, hbm, vmem],
        out_specs=[hbm] * 4 + [vmem] * 2,
        scratch_shapes=[
            pltpu.VMEM((patches, width), bf),
            pltpu.VMEM((patches, width), bf),
            pltpu.VMEM((patches, nk), bf),
            pltpu.VMEM((patches, nk), bf),
            pltpu.VMEM((8, width), f32),
            pltpu.VMEM((2, nblk, rows, width), bf),
            pltpu.VMEM((2, nrow, 8, 128), f32),
            pltpu.VMEM((2, nt - 1, nrow, 8, 128), f32),
            pltpu.VMEM((2, nblk, rows, width), f32),
            pltpu.VMEM((2, rows, width), f32),
            pltpu.VMEM((ndp, 2, rows, width), bf),
            pltpu.VMEM((ndp, 2, rows, width), bf),
            pltpu.VMEM((rows, width), bf),
            pltpu.VMEM((rows, width), bf),
            pltpu.VMEM((ndp, rows, width), bf),
            pltpu.VMEM((ndp, rows, width), bf),
            pltpu.VMEM((ndp, rows, width), bf),
            pltpu.VMEM((ndp, rows, width), bf),
            pltpu.VMEM((nt, patches, HD), f32),
            pltpu.VMEM((nt - 1, patches, HD), bf),
            pltpu.VMEM((patches, width), f32),
            pltpu.VMEM((patches, width), bf),
            pltpu.VMEM((patches, width), bf),
            pltpu.VMEM((nk, patches), bf),
            pltpu.VMEM((nk, patches), bf),
            pltpu.VMEM((nt - 1, patches, HD), bf),
            pltpu.VMEM((2, patches, HD), bf),
            pltpu.VMEM((2, patches, HD), bf),
            dma((7,)), dma((2,)), dma((4,)),
            dma((2, 6 * ndp)), dma((2, nblk)),
            dma((2, nt - 1)), dma((2, nt - 1)),
            dma((ndp,)), dma((ndp,)), dma((ndp,)), dma((ndp,)),
            dma((ndp,)), dma((ndp,)), dma((ndp,)), dma((ndp,)),
            dma((ndp,)), dma((ndp,)), dma((1,)), dma((1,)),
            dma((nt - 1,)), dma((nt - 1,)), dma((2,)), dma((2,)),
        ],
        compiler_params=pltpu.CompilerParams(
            collective_id=0, has_side_effects=True, vmem_limit_bytes=60 * 1024 * 1024
        ),
    )(states, resid, up, gain, vw, ow, ctx, q, starts)


GROUP = 4


def byte_kernel(
    tab, bounds, g, q, wgv_in, wgo_in, keys_in, values_in, gk_out, gv_out, wgv, wgo,
    keys, values, gk, gv, expo, pgrad, bd, sums, table, s_k, s_v, o_k, o_v, s_w,
):
    total = g.shape[0]
    nwin = total // WIN
    nbytes = keys.shape[0]
    chunk = GROUP * BLK
    nchunk = nbytes // chunk
    lag = 1 + -(-(nwin - 1) // GROUP)
    ngroup = expo.shape[0] // GROUP
    scale = 1.0 / math.sqrt(HD)

    def rows_of(c):
        return pl.ds(pl.multiple_of(c * chunk, chunk), chunk)

    def load(c):
        here = rows_of(c)
        return (
            pltpu.make_async_copy(keys_in.at[here], keys.at[here], s_k.at[c]),
            pltpu.make_async_copy(values_in.at[here], values.at[here], s_v.at[c]),
        )

    def store(c):
        here = rows_of(c)
        return (
            pltpu.make_async_copy(gk.at[here], gk_out.at[here], o_k.at[c]),
            pltpu.make_async_copy(gv.at[here], gv_out.at[here], o_v.at[c]),
        )

    for c in range(nchunk):
        for x in load(c):
            x.start()
    passed = (
        pltpu.make_async_copy(wgv_in, wgv, s_w.at[0]),
        pltpu.make_async_copy(wgo_in, wgo, s_w.at[1]),
    )
    for x in passed:
        x.start()

    zero = jnp.zeros((WIN, HD), jnp.bfloat16)
    for w in range(nwin):
        bd[w, :WIN, :HD] = q[w * WIN : (w + 1) * WIN, :]
        bd[w, WIN:, HD:] = g[w * WIN : (w + 1) * WIN, :]
        bd[w, :WIN, HD:] = zero
        bd[w, WIN:, :HD] = zero
    bd[nwin] = jnp.zeros((2 * WIN, 2 * HD), jnp.bfloat16)
    sums[...] = jnp.zeros_like(sums)
    row = lax.broadcasted_iota(jnp.int32, (BLK, WIN), 0)

    def place(n):
        b, w = tab[0, n], tab[1, n]
        return (
            b, w, pl.ds(pl.multiple_of(b * BLK, BLK), BLK), pl.ds(pl.multiple_of(w * WIN, WIN), WIN)
        )

    def measure(group, _):
        @pl.when(group < nchunk)
        def _():
            for x in load(group):
                x.wait()

        for k in range(GROUP):
            n = group * GROUP + k
            b, w, here, lanes = place(n)
            both = jnp.concatenate([keys[here, :], values[here, :]], axis=1)
            s = lax.dot_general(
                both, bd[w], (((1,), (1,)), ((), ())), preferred_element_type=jnp.float32
            )
            lo = bounds[0:1, lanes] - b * BLK
            hi = bounds[1:2, lanes] - b * BLK
            e = jnp.where((row >= lo) & (row < hi), jnp.exp(s[:, :WIN] * scale), 0.0)
            pg = s[:, WIN:]
            expo[n] = e
            pgrad[n] = pg
            sums[0:1, lanes] += jnp.sum(e, axis=0, keepdims=True)
            sums[1:2, lanes] += jnp.sum(e * pg, axis=0, keepdims=True)
        return 0

    lax.fori_loop(0, ngroup, measure, 0)
    t = sums[0:1, :]
    inv = jnp.where(t > 0.0, 1.0 / jnp.where(t > 0.0, t, 1.0), 0.0)
    table[0:1, :] = inv
    table[1:2, :] = sums[1:2, :] * inv

    def apply(group, _):
        for k in range(GROUP):
            n = group * GROUP + k
            b, w, here, lanes = place(n)
            fresh = (n == 0) | (tab[0, jnp.maximum(n - 1, 0)] != b)
            p = expo[n] * table[0:1, lanes]
            sg = p * (pgrad[n] - table[1:2, lanes]) * scale
            both = jnp.concatenate([sg.astype(jnp.bfloat16), p.astype(jnp.bfloat16)], axis=1)
            out = jnp.dot(both, bd[w], preferred_element_type=jnp.float32).astype(jnp.bfloat16)

            @pl.when(fresh)
            def _():
                gk[here, :] = out[:, :HD]
                gv[here, :] = out[:, HD:]

            @pl.when(jnp.logical_not(fresh))
            def _():
                gk[here, :] += out[:, :HD]
                gv[here, :] += out[:, HD:]

        @pl.when((group >= lag) & (group - lag < nchunk))
        def _():
            for x in store(group - lag):
                x.start()

        return 0

    lax.fori_loop(0, ngroup, apply, 0)
    for c in range(max(ngroup - lag, 0), nchunk):
        for x in store(c):
            x.start()
    for c in range(nchunk):
        for x in store(c):
            x.wait()
    for x in passed:
        x.wait()


def byte_call(tab, bounds, g, q, wgv, wgo, keys, values):
    bf, f32 = jnp.bfloat16, jnp.float32
    nbytes = keys.shape[0]
    total = g.shape[0]
    nwin = total // WIN
    npair = -(-(nbytes // BLK + nwin - 1) // GROUP) * GROUP
    nchunk = nbytes // (GROUP * BLK)
    vmem = pl.BlockSpec(memory_space=pltpu.VMEM)
    hbm = pl.BlockSpec(memory_space=pl.ANY)
    dma = pltpu.SemaphoreType.DMA
    return pl.pallas_call(
        byte_kernel,
        out_shape=(
            jax.ShapeDtypeStruct(keys.shape, bf),
            jax.ShapeDtypeStruct(keys.shape, bf),
            jax.ShapeDtypeStruct(wgv.shape, f32),
            jax.ShapeDtypeStruct(wgo.shape, f32),
        ),
        in_specs=[pl.BlockSpec(memory_space=pltpu.SMEM), vmem, vmem, vmem] + [hbm] * 4,
        out_specs=[hbm] * 4,
        scratch_shapes=[
            pltpu.VMEM(keys.shape, bf), pltpu.VMEM(keys.shape, bf),
            pltpu.VMEM(keys.shape, bf), pltpu.VMEM(keys.shape, bf),
            pltpu.VMEM((npair, BLK, WIN), f32), pltpu.VMEM((npair, BLK, WIN), f32),
            pltpu.VMEM((nwin + 1, 2 * WIN, 2 * HD), bf),
            pltpu.VMEM((8, total + WIN), f32), pltpu.VMEM((8, total + WIN), f32),
            dma((nchunk,)), dma((nchunk,)), dma((nchunk,)), dma((nchunk,)), dma((2,)),
        ],
        compiler_params=pltpu.CompilerParams(vmem_limit_bytes=60 * 1024 * 1024),
    )(tab, bounds, g, q, wgv, wgo, keys, values)


def on_device_kernels(
    ndp, nt, patch_states, residual_grad, upstream_value, norm_gain, value_weight, out_weight,
    attn_out, queries, byte_keys, byte_values, patch_starts,
):
    nbytes = byte_keys.shape[1]
    wgv, wgo, g, q, tab, bounds = grad_call(
        ndp, nt, nbytes, patch_states[0], residual_grad[0], upstream_value[0],
        norm_gain.reshape(-1, 128), value_weight, out_weight, attn_out[0], queries[0], patch_starts,
    )
    gk, gv, wgv, wgo = byte_call(
        tab, bounds, g.reshape(-1, HD), q.reshape(-1, HD), wgv, wgo, byte_keys[0], byte_values[0]
    )
    return (wgv, wgo, gk[None], gv[None])


def solution(mesh):
    ndp, nseq, nt = mesh.shape["dp"], mesh.shape["seq"], mesh.shape["tensor"]
    use_kernels = nseq == 2 and ndp == 4
    body = functools.partial(on_device_kernels, ndp, nt) if use_kernels else on_device
    return jax.shard_map(
        body,
        mesh=mesh,
        in_specs=(
            P("dp", "seq", "tensor"),
            P("dp", "seq", "tensor"),
            P("dp", "seq", None),
            P("tensor"),
            P(("dp", "seq"), "tensor"),
            P(("dp", "seq"), "tensor"),
            P("dp", "seq", None),
            P("dp", "seq", "tensor"),
            P("dp", "seq", "tensor"),
            P("dp", "seq", "tensor"),
            P("dp", None),
        ),
        out_specs=(
            P(("dp", "seq"), "tensor"),
            P(("dp", "seq"), "tensor"),
            P("dp", "seq", "tensor"),
            P("dp", "seq", "tensor"),
        ),
        check_vma=False,
    )
```

time: 102 us -> 80.3 us (0.79); the launches traced: 100 us -> 80 us
  Pallas kernels: 89.2 us -> 79.4 us
  local copies, waits for them, and re-layouts: 9.23 us -> 0 us
  other arithmetic: 1.37 us -> 0 us
    pallas_call x1 -> x2, Pallas kernels: 89.2 us -> 79.4 us  [the longest x1 61 us: grad_call(): pl.pallas_call(functools.partial(grad_kernel, ndp, nt, nbytes), out_shape...]
    unnamed x6 -> x0, local copies, waits for them, and re-layouts: 7.86 us -> none
    broadcast_in_dim x1 -> x0, local copies, waits for them, and re-layouts: 1.28 us -> none  [on_device_kernels(): norm_gain[None]]
where the time goes in v1:
time: 80.3 us; the launch traced here: 80 us
  Pallas kernels  79.4 us (99%)
    pallas_call x1, Pallas kernels, grad_call(): pl.pallas_call(functools.partial(grad_kernel, ndp, nt, nbytes), out_shape...  61 us
    pallas_call x1, Pallas kernels, byte_call(): pl.pallas_call(byte_kernel, out_shape=(jax.ShapeDtypeStruct(keys.shape, b...  18.4 us

profile of v1, /device:TPU:0, one launch (start us, length us, event | category | flops | bytes accessed | tf_op | source)
XLA Modules:
  0.0 80.0 jit_solution(11877708941492804646)
XLA Ops:
  0.6 61.0 %shard_map.138 = (f32[64,1024]{1,0:T(8,128)}, f32[64,1024]{1,0:T(8,128)}, bf16[2,384,128]{2,1,0:T(8,128)(2,1)}, bf16[2,384,128]{2,1,0:T(8,128)(2,1)}, s32[2,128]{1,0:T(2,128)}, /*index=5*/s32[2,896]{1,0:T(2,128)}) custom-call(bf16[384,1024]{1,0:T(8,128)(2,1)} %bitcast.14, bf16[384,1024]{1,0:T(8,128)(2,1)} %bitcast.15, bf16[384,512]{1,0:T(8,128)(2,1)} %bitcast.16, ...), custom_call_target="tpu_custom_call" | custom-call | tf_op jit(solution)/shard_map/pallas_call | solution.py:501
  61.7 18.4 %shard_map.139 = (bf16[8192,128]{1,0:T(8,128)(2,1)}, bf16[8192,128]{1,0:T(8,128)(2,1)}, f32[64,1024]{1,0:T(8,128)}, f32[64,1024]{1,0:T(8,128)}) custom-call(s32[2,128]{1,0:T(2,128)} %get-tuple-element.14.tab, s32[2,896]{1,0:T(2,128)} %get-tuple-element.15.bounds, bf16[768,128]{1,0:T(8,128)(2,1)} %bitcast.18, bf16[768,128]{1,0:T(8,128)(2,1)} %bitcast.19, ...), custom_call_target="tpu_custom_call" | custom-call | tf_op jit(solution)/shard_map/pallas_call | solution.py:692

commit v2 on v1

--- a/solution.py
+++ b/solution.py
@@ -163,10 +163,10 @@
 def grad_kernel(
     ndp, nt, nbytes, states_in, resid_in, up_in, gain_in, vw, ow, ctx_in, q_in, starts,
     wgv, wgo, g_out, q_out, tab, bounds,
-    states, resid, up, ctx, gain, wall, sqs, sqr, part, acc, rbv, lbv, ysv, yrv, rbo, lbo, yso, yro,
+    states, resid, up, ctx, gain, wall, sqs, sqr, part, acc, acco, accz, rbz, lbz, ysz, yrz, rbv, lbv, ysv, yrv, rbo, lbo, yso, yro,
     pas, par, gn, nrm, gpat, trans_v, trans_o, gsend, gboth, qboth,
     s_in, s_own, s_out, s_ag, r_ag, s_sq, r_sq, s_rv, r_rv, s_lv, r_lv, s_ro, r_ro, s_lo, r_lo,
-    s_yo, r_yo, s_yv, r_yv, s_pa, r_pa, s_g, r_g,
+    s_rz, r_rz, s_lz, r_lz, s_yo, r_yo, s_yv, r_yv, s_pa, r_pa, s_g, r_g,
 ):
     dp, sq, tn = lax.axis_index("dp"), lax.axis_index("seq"), lax.axis_index("tensor")
     patches, width = states.shape
@@ -217,30 +217,49 @@
 
     weights = (vw, ow)
 
-    def shard(w, zz, yy, dev, k, own=False):
+    def half(h):
+        return pl.ds(h * (vw.shape[0] // 2), vw.shape[0] // 2)
+
+    def shard(w, zz, yy, h, dev, k, own=False):
         slot = zz * 2 + yy
-        src = weights[w] if own else wall.at[w, slot]
-        return copy(src, wall.at[w, slot], s_ag.at[w, k], r_ag.at[w, slot], dev)
-
-    def ag_own_z(w):
-        go(shard(w, dp, sq, right, 0, True), dp < last)
-        go(shard(w, dp, sq, left, 1, True), dp > 0)
-
-    def ag_own_y(w):
-        go(shard(w, dp, sq, ydev, 2, True))
-
-    def ag_forward(w, s):
+        block = wall.at[w, slot, half(h)]
+        src = weights[w].at[half(h)] if own else block
+        return copy(src, block, s_ag.at[w, h, k], r_ag.at[w, h, slot], dev)
+
+    def ag_own_z(w, h, ends=True, inner=True):
+        for dev, onward, edge, k in ((right, dp < last, dp == 0, 0), (left, dp > 0, dp == last, 1)):
+            if ends:
+                go(shard(w, dp, sq, h, dev, k, True), edge)
+            if inner:
+                go(shard(w, dp, sq, h, dev, k, True), onward & jnp.logical_not(edge))
+
+    def ag_own_y(w, h):
+        go(shard(w, dp, sq, h, ydev, 2, True))
+
+    def ag_forward(w, s, h):
         for zz, here, dev, onward, k in (
             (dp - s, dp - s >= 0, right, dp < last, 3 * s),
             (dp + s, dp + s <= last, left, dp > 0, 3 * ndp + 3 * s),
         ):
-            pl.when(here)(shard(w, zz, sq, dev, k).wait_recv)
-            go(shard(w, zz, sq, dev, k), here & onward)
-            go(shard(w, zz, sq, ydev, k + 1), here)
+            pl.when(here)(shard(w, zz, sq, h, dev, k).wait_recv)
+            go(shard(w, zz, sq, h, dev, k), here & onward)
+            spread = here if w == 0 or s > 1 else here & ((zz == 0) | (zz == last))
+            go(shard(w, zz, sq, h, ydev, k + 1), spread)
+
+    def ag_cross(w, h):
+        inner = (dp > 0) & (dp < last)
+        pl.when(inner)(shard(w, dp, 1 - sq, h, ydev, 2).wait_recv)
+        go(shard(w, dp, 1 - sq, h, right, 11), inner)
+        go(shard(w, dp, 1 - sq, h, left, 12), inner)
 
     def ag_wait_y(w):
         for zz in range(ndp):
-            shard(w, zz, 1 - sq, ydev, 2).wait_recv()
+            for h in range(2):
+                wait = shard(w, zz, 1 - sq, h, ydev, 2).wait_recv
+                if w == 0 or zz in (0, last):
+                    wait()
+                else:
+                    pl.when(dp != zz)(wait)
 
     def row_loop(fn):
         def body(i, _):
@@ -287,62 +306,77 @@
 
         lax.fori_loop(0, ncol, body, 0)
 
-    def two(zz):
-        return part[0, pl.ds(zz * 2, 2)]
-
-    def one(zz):
-        yo(zz).wait_recv()
-        return part[1, zz * 2 + sq] + yro[zz].astype(jnp.float32)
-
-    def line(d, get, buf_r, buf_l, s_r, r_r, s_l, r_l):
+    def part_v(zz, h):
+        return part[0, zz * 2 + h]
+
+    def part_z(zz, h):
+        return part[1, zz * 2 + h, half(1)]
+
+    def part_o(zz, h):
+        yo(zz, h).wait_recv()
+        return part[1, zz * 2 + sq, half(h)] + yro[zz, h].astype(jnp.float32)
+
+    def hops(d, h, buf_r, buf_l, s_r, r_r, s_l, r_l):
         for zz, valid, dev, fed, buf, ss, rs in (
             (dp + d, dp + d <= last, right, dp > 0, buf_r, s_r, r_r),
             (dp - d, dp - d >= 0, left, dp < last, buf_l, s_l, r_l),
         ):
-            c = copy(buf.at[zz], buf.at[zz], ss.at[d - 1], rs.at[zz], dev)
-
-            @pl.when(valid)
-            def _(zz=zz, fed=fed, buf=buf, c=c):
-                mine_part = get(zz)
-
-                @pl.when(fed)
-                def _():
-                    c.wait_recv()
-                    buf[zz] = (mine_part + buf[zz].astype(jnp.float32)).astype(jnp.bfloat16)
-
-                @pl.when(jnp.logical_not(fed))
-                def _():
-                    buf[zz] = mine_part.astype(jnp.bfloat16)
-
-            go(c, valid)
-
-    def line_end(rows, buf_r, buf_l, s_r, r_r, s_l, r_l):
+            c = copy(buf.at[zz, h], buf.at[zz, h], ss.at[d - 1, h], rs.at[zz, h], dev)
+            yield zz, valid, fed, buf, c
+
+    def line_open(get, bufs, halves=(0, 1)):
+        for d in range(last, 0, -1):
+            for h in halves:
+                for zz, valid, fed, buf, c in hops(d, h, *bufs):
+                    opening = valid & jnp.logical_not(fed)
+
+                    @pl.when(opening)
+                    def _(zz=zz, h=h, buf=buf):
+                        buf[zz, h] = get(zz, h).astype(jnp.bfloat16)
+
+                    go(c, opening)
+
+    def line(d, h, get, bufs):
+        for zz, valid, fed, buf, c in hops(d, h, *bufs):
+
+            @pl.when(valid & fed)
+            def _(zz=zz, buf=buf, c=c):
+                mine_part = get(zz, h)
+                c.wait_recv()
+                buf[zz, h] = (mine_part + buf[zz, h].astype(jnp.float32)).astype(jnp.bfloat16)
+
+            go(c, valid & fed)
+
+    def line_end(h, acc, bufs):
+        buf_r, buf_l, s_r, r_r, s_l, r_l = bufs
         for fed, dev, buf, ss, rs in (
             (dp > 0, right, buf_r, s_r, r_r),
             (dp < last, left, buf_l, s_l, r_l),
         ):
-            c = copy(buf.at[dp], buf.at[dp], ss.at[0], rs.at[dp], dev)
+            c = copy(buf.at[dp, h], buf.at[dp, h], ss.at[0, h], rs.at[dp, h], dev)
 
             @pl.when(fed)
             def _(c=c, buf=buf):
                 c.wait_recv()
-                acc[rows] += buf[dp].astype(jnp.float32)
+                acc[h] += buf[dp, h].astype(jnp.float32)
 
     line_v = (rbv, lbv, s_rv, r_rv, s_lv, r_lv)
     line_o = (rbo, lbo, s_ro, r_ro, s_lo, r_lo)
-
-    def yo(zz):
-        return copy(yso.at[zz], yro.at[zz], s_yo.at[zz], r_yo.at[zz], ydev)
-
-    def send_yo(zz, cond=None):
+    line_z = (rbz, lbz, s_rz, r_rz, s_lz, r_lz)
+
+    def yo(zz, h):
+        return copy(yso.at[zz, h], yro.at[zz, h], s_yo.at[zz, h], r_yo.at[zz, h], ydev)
+
+    def send_yo(zz, h, cond=None):
         def fill():
-            yso[zz] = part[1, zz * 2 + (1 - sq)].astype(jnp.bfloat16)
+            yso[zz, h] = part[1, zz * 2 + (1 - sq), half(h)].astype(jnp.bfloat16)
 
         fill() if cond is None else pl.when(cond)(fill)
-        go(yo(zz), cond)
-
-    ag_own_z(0)
-    ag_own_y(0)
+        go(yo(zz, h), cond)
+
+    for h in range(2):
+        ag_own_z(0, h)
+        ag_own_y(0, h)
     for i in range(width // 128):
         gain[:, i * 128 : (i + 1) * 128] = jnp.broadcast_to(
             gain_in[i : i + 1, :].astype(jnp.float32), (8, 128)
@@ -365,13 +399,16 @@
     bounds[0:1, first.shape[1] :] = far
     bounds[1:2, first.shape[1] :] = far
 
-    ag_forward(0, 1)
+    ag_forward(0, 1, 0)
     for c in sq_copies:
         c.wait_recv()
     row_loop(normalise)
+    ag_forward(0, 1, 1)
     wgrad(0, trans_v, nrm)
-    line(3, two, *line_v)
-
+    for h in range(2):
+        ag_own_z(1, h, inner=False)
+    line_open(part_v, line_v)
+    ag_forward(0, 2, 0)
     nblocks = nbytes // BLK
     ends = lax.broadcasted_iota(jnp.int32, (nblocks, first.shape[1]), 0) * BLK + (BLK - 1)
     reach = (jnp.broadcast_to(first, ends.shape) <= ends).astype(jnp.int32)
@@ -385,16 +422,17 @@
     tab[0:1, :] = jnp.where(done, nblocks - 1, block_of)
     tab[1:2, :] = jnp.where(done, first.shape[1] // WIN, window)
 
-    ag_forward(0, 2)
-    ag_own_z(1)
-    ag_forward(0, 3)
-    ag_own_y(1)
+    ag_forward(0, 2, 1)
     local["ctx"].wait()
     trans_o[...] = ctx[...].T
-    line(2, two, *line_v)
-    ag_forward(1, 1)
+    for h in range(2):
+        ag_forward(0, 3, h)
+        ag_own_z(1, h, ends=False)
+        ag_own_y(1, h)
+    ag_forward(1, 1, 0)
     local["vw"].wait()
     ag_wait_y(0)
+    ag_forward(1, 1, 1)
 
     def project(here, i):
         full = wall[0].reshape(up.shape[1], width)
@@ -405,8 +443,12 @@
 
     row_loop(project)
     cr_copies = share(1)
-    ag_forward(1, 2)
-    line(1, two, *line_v)
+    ag_cross(1, 0)
+    ag_forward(1, 2, 0)
+    ag_cross(1, 1)
+    line(2, 0, part_v, line_v)
+    ag_forward(1, 2, 1)
+    line(2, 1, part_v, line_v)
     local["resid"].wait()
     for c in cr_copies:
         c.wait_recv()
@@ -422,58 +464,78 @@
         ).astype(jnp.bfloat16)
 
     row_loop(make_grad)
-    ag_forward(1, 3)
-    wgrad(1, trans_o, gpat)
+    ag_forward(1, 3, 0)
+    ag_forward(1, 3, 1)
     local["q"].wait()
     qc = go(copy(qboth.at[sq], qboth.at[sq], s_g.at[0], r_g.at[0], ydev))
+    wgrad(1, trans_o, gpat)
+    line_open(part_z, line_z)
     for k in range(ndp - 1, 0, -1):
-        send_yo(dp + k, dp + k <= last)
-        send_yo(dp - k, dp - k >= 0)
-    send_yo(dp)
+        send_yo(dp + k, 0, dp + k <= last)
+        send_yo(dp - k, 0, dp - k >= 0)
+    send_yo(dp, 0)
+    for h in range(2):
+        line(1, h, part_v, line_v)
+    for h in range(2):
+        line(2, h, part_z, line_z)
     local["ow"].wait()
     ag_wait_y(1)
 
-    def attn(here, i):
+    def tile(i):
+        return pl.ds(i * tall, tall)
+
+    def pa(i, k):
+        return copy(gsend.at[k - 1, tile(i)], par.at[k - 1, tile(i)], s_pa.at[k - 1, i],
+                    r_pa.at[k - 1, i], tdev(k))
+
+    for i in range(nrow):
         full = wall[1].reshape(up.shape[1], width)
         p = lax.dot_general(
-            gpat[here, :], full, (((1,), (1,)), ((), ())), preferred_element_type=jnp.float32
+            gpat[tile(i), :], full, (((1,), (1,)), ((), ())), preferred_element_type=jnp.float32
         )
         for j in range(nt):
-            pas[j, here, :] = p[:, j * HD : (j + 1) * HD]
-
-    row_loop(attn)
-    pa_copies = []
-    for k in range(1, nt):
-        gsend[k - 1] = pas[lax.rem(tn + k, nt)].astype(jnp.bfloat16)
-        pa_copies.append(
-            go(copy(gsend.at[k - 1], par.at[k - 1], s_pa.at[k - 1], r_pa.at[k - 1], tdev(k)))
-        )
-
-    acc[...] = two(dp)
-    line_end(pl.ds(0, 2), *line_v)
+            pas[j, tile(i), :] = p[:, j * HD : (j + 1) * HD]
+        for k in range(1, nt):
+            gsend[k - 1, tile(i)] = pas[lax.rem(tn + k, nt), tile(i)].astype(jnp.bfloat16)
+            go(pa(i, k))
+
+    for h in range(2):
+        acc[h] = part_v(dp, h)
+        line_end(h, acc, line_v)
     ysv[...] = acc[1 - sq].astype(jnp.bfloat16)
     yv = go(copy(ysv, yrv, s_yv.at[0], r_yv.at[0], ydev))
-
-    total = pas[tn]
-    for k, c in enumerate(pa_copies):
-        c.wait_recv()
-        total = total + par[k].astype(jnp.float32)
-    gboth[sq] = total.astype(jnp.bfloat16)
-    gc = go(copy(gboth.at[sq], gboth.at[sq], s_g.at[1], r_g.at[1], ydev))
-
-    line(3, one, *line_o)
-    line(2, one, *line_o)
+    line_open(part_o, line_o, (0,))
+    for h in range(2):
+        line(1, h, part_z, line_z)
+    line(2, 0, part_o, line_o)
+    gc = []
+    for i in range(nrow):
+        total = pas[tn, tile(i)]
+        for k in range(1, nt):
+            pa(i, k).wait_recv()
+            total = total + par[k - 1, tile(i)].astype(jnp.float32)
+        gboth[sq, tile(i)] = total.astype(jnp.bfloat16)
+        block = gboth.at[sq, tile(i)]
+        gc.append(go(copy(block, block, s_g.at[1 + i], r_g.at[1 + i], ydev)))
+    for h in range(2):
+        accz[h] = part_z(dp, h)
+        line_end(h, accz, line_z)
+    ysz[...] = accz[1 - sq].astype(jnp.bfloat16)
+    yz = go(copy(ysz, yrz, s_yv.at[1], r_yv.at[1], ydev))
+    line(1, 0, part_o, line_o)
     yv.wait_recv()
     acc[0] = acc[sq] + yrv[...].astype(jnp.float32)
     out_v = pltpu.make_async_copy(acc.at[0], wgv, s_out.at[0])
     out_v.start()
-    line(1, one, *line_o)
-    acc[1] = one(dp)
-    line_end(1, *line_o)
-    out_o = pltpu.make_async_copy(acc.at[1], wgo, s_out.at[1])
+    acco[0] = part_o(dp, 0)
+    line_end(0, acco, line_o)
+    yz.wait_recv()
+    acco[1] = accz[sq] + yrz[...].astype(jnp.float32)
+    out_o = pltpu.make_async_copy(acco, wgo, s_out.at[1])
     out_o.start()
     qc.wait_recv()
-    gc.wait_recv()
+    for c in gc:
+        c.wait_recv()
     out_q = pltpu.make_async_copy(qboth, q_out, s_out.at[2])
     out_q.start()
     out_g = pltpu.make_async_copy(gboth, g_out, s_out.at[3])
@@ -502,7 +564,7 @@
         functools.partial(grad_kernel, ndp, nt, nbytes),
         out_shape=(
             jax.ShapeDtypeStruct((rows, width), f32),
-            jax.ShapeDtypeStruct((rows, width), f32),
+            jax.ShapeDtypeStruct((2, rows // 2, width), f32),
             jax.ShapeDtypeStruct((2, patches, HD), bf),
             jax.ShapeDtypeStruct((2, patches, HD), bf),
             jax.ShapeDtypeStruct((2, 128), i32),
@@ -521,14 +583,20 @@
             pltpu.VMEM((2, nt - 1, nrow, 8, 128), f32),
             pltpu.VMEM((2, nblk, rows, width), f32),
             pltpu.VMEM((2, rows, width), f32),
+            pltpu.VMEM((2, rows // 2, width), f32),
+            pltpu.VMEM((2, rows // 2, width), f32),
+            pltpu.VMEM((ndp, 2, rows // 2, width), bf),
+            pltpu.VMEM((ndp, 2, rows // 2, width), bf),
+            pltpu.VMEM((rows // 2, width), bf),
+            pltpu.VMEM((rows // 2, width), bf),
             pltpu.VMEM((ndp, 2, rows, width), bf),
             pltpu.VMEM((ndp, 2, rows, width), bf),
             pltpu.VMEM((rows, width), bf),
             pltpu.VMEM((rows, width), bf),
-            pltpu.VMEM((ndp, rows, width), bf),
-            pltpu.VMEM((ndp, rows, width), bf),
-            pltpu.VMEM((ndp, rows, width), bf),
-            pltpu.VMEM((ndp, rows, width), bf),
+            pltpu.VMEM((ndp, 2, rows // 2, width), bf),
+            pltpu.VMEM((ndp, 2, rows // 2, width), bf),
+            pltpu.VMEM((ndp, 2, rows // 2, width), bf),
+            pltpu.VMEM((ndp, 2, rows // 2, width), bf),
             pltpu.VMEM((nt, patches, HD), f32),
             pltpu.VMEM((nt - 1, patches, HD), bf),
             pltpu.VMEM((patches, width), f32),
@@ -540,12 +608,13 @@
             pltpu.VMEM((2, patches, HD), bf),
             pltpu.VMEM((2, patches, HD), bf),
             dma((7,)), dma((2,)), dma((4,)),
-            dma((2, 6 * ndp)), dma((2, nblk)),
+            dma((2, 2, 6 * ndp)), dma((2, 2, nblk)),
             dma((2, nt - 1)), dma((2, nt - 1)),
-            dma((ndp,)), dma((ndp,)), dma((ndp,)), dma((ndp,)),
-            dma((ndp,)), dma((ndp,)), dma((ndp,)), dma((ndp,)),
-            dma((ndp,)), dma((ndp,)), dma((1,)), dma((1,)),
-            dma((nt - 1,)), dma((nt - 1,)), dma((2,)), dma((2,)),
+            dma((ndp, 2)), dma((ndp, 2)), dma((ndp, 2)), dma((ndp, 2)),
+            dma((ndp, 2)), dma((ndp, 2)), dma((ndp, 2)), dma((ndp, 2)),
+            dma((ndp, 2)), dma((ndp, 2)), dma((ndp, 2)), dma((ndp, 2)),
+            dma((ndp, 2)), dma((ndp, 2)), dma((2,)), dma((2,)),
+            dma((nt - 1, nrow)), dma((nt - 1, nrow)), dma((1 + nrow,)), dma((1 + nrow,)),
         ],
         compiler_params=pltpu.CompilerParams(
             collective_id=0, has_side_effects=True, vmem_limit_bytes=60 * 1024 * 1024
@@ -553,12 +622,12 @@
     )(states, resid, up, gain, vw, ow, ctx, q, starts)
 
 
-GROUP = 4
+GROUP = 8
 
 
 def byte_kernel(
     tab, bounds, g, q, wgv_in, wgo_in, keys_in, values_in, gk_out, gv_out, wgv, wgo,
-    keys, values, gk, gv, expo, pgrad, bd, sums, table, s_k, s_v, o_k, o_v, s_w,
+    keys, values, gk, gv, expo, pgrad, bd, sums, table, held, s_k, s_v, o_k, o_v, s_w,
 ):
     total = g.shape[0]
     nwin = total // WIN
@@ -589,11 +658,10 @@
     for c in range(nchunk):
         for x in load(c):
             x.start()
-    passed = (
-        pltpu.make_async_copy(wgv_in, wgv, s_w.at[0]),
-        pltpu.make_async_copy(wgo_in, wgo, s_w.at[1]),
-    )
-    for x in passed:
+    carried = ((wgv_in, wgv), (wgo_in, wgo))
+    taken = [pltpu.make_async_copy(a, held.at[i], s_w.at[i]) for i, (a, _) in enumerate(carried)]
+    passed = [pltpu.make_async_copy(held.at[i], b, s_w.at[2 + i]) for i, (_, b) in enumerate(carried)]
+    for x in taken:
         x.start()
 
     zero = jnp.zeros((WIN, HD), jnp.bfloat16)
@@ -636,30 +704,32 @@
         return 0
 
     lax.fori_loop(0, ngroup, measure, 0)
+    for x, y in zip(taken, passed):
+        x.wait()
+        y.start()
     t = sums[0:1, :]
     inv = jnp.where(t > 0.0, 1.0 / jnp.where(t > 0.0, t, 1.0), 0.0)
     table[0:1, :] = inv
     table[1:2, :] = sums[1:2, :] * inv
 
     def apply(group, _):
+        first = group * GROUP
+        prior = jnp.maximum(first - 1, 0)
+        before = pl.ds(pl.multiple_of(tab[0, prior] * BLK, BLK), BLK)
+        held_k, held_v = gk[before, :], gv[before, :]
         for k in range(GROUP):
-            n = group * GROUP + k
+            n = first + k
             b, w, here, lanes = place(n)
-            fresh = (n == 0) | (tab[0, jnp.maximum(n - 1, 0)] != b)
+            same = tab[0, jnp.maximum(n - 1, 0)] == b
+            same = same & (n > 0) if k == 0 else same
             p = expo[n] * table[0:1, lanes]
             sg = p * (pgrad[n] - table[1:2, lanes]) * scale
             both = jnp.concatenate([sg.astype(jnp.bfloat16), p.astype(jnp.bfloat16)], axis=1)
             out = jnp.dot(both, bd[w], preferred_element_type=jnp.float32).astype(jnp.bfloat16)
-
-            @pl.when(fresh)
-            def _():
-                gk[here, :] = out[:, :HD]
-                gv[here, :] = out[:, HD:]
-
-            @pl.when(jnp.logical_not(fresh))
-            def _():
-                gk[here, :] += out[:, :HD]
-                gv[here, :] += out[:, HD:]
+            held_k = out[:, :HD] + jnp.where(same, held_k, jnp.zeros_like(held_k))
+            held_v = out[:, HD:] + jnp.where(same, held_v, jnp.zeros_like(held_v))
+            gk[here, :] = held_k
+            gv[here, :] = held_v
 
         @pl.when((group >= lag) & (group - lag < nchunk))
         def _():
@@ -705,7 +775,8 @@
             pltpu.VMEM((npair, BLK, WIN), f32), pltpu.VMEM((npair, BLK, WIN), f32),
             pltpu.VMEM((nwin + 1, 2 * WIN, 2 * HD), bf),
             pltpu.VMEM((8, total + WIN), f32), pltpu.VMEM((8, total + WIN), f32),
-            dma((nchunk,)), dma((nchunk,)), dma((nchunk,)), dma((nchunk,)), dma((2,)),
+            pltpu.VMEM((2,) + wgv.shape, f32),
+            dma((nchunk,)), dma((nchunk,)), dma((nchunk,)), dma((nchunk,)), dma((4,)),
         ],
         compiler_params=pltpu.CompilerParams(vmem_limit_bytes=60 * 1024 * 1024),
     )(tab, bounds, g, q, wgv, wgo, keys, values)
@@ -721,7 +792,7 @@
         norm_gain.reshape(-1, 128), value_weight, out_weight, attn_out[0], queries[0], patch_starts,
     )
     gk, gv, wgv, wgo = byte_call(
-        tab, bounds, g.reshape(-1, HD), q.reshape(-1, HD), wgv, wgo, byte_keys[0], byte_values[0]
+        tab, bounds, g.reshape(-1, HD), q.reshape(-1, HD), wgv, wgo.reshape(wgv.shape), byte_keys[0], byte_values[0]
     )
     return (wgv, wgo, gk[None], gv[None])
 

time: 80.3 us -> 64.8 us (0.81)
  Pallas kernels: 79.4 us -> 64 us
    pallas_call x1, Pallas kernels: 18.4 us -> 9.71 us  [byte_call(): pl.pallas_call(byte_kernel, out_shape=(jax.ShapeDtypeStruct(keys.shape, b...]
    pallas_call x1, Pallas kernels: 61 us -> 54.3 us  [grad_call(): pl.pallas_call(functools.partial(grad_kernel, ndp, nt, nbytes), out_shape...]
where the time goes in v2:
time: 64.8 us; the launch traced here: 64.6 us
  Pallas kernels  64 us (99%)
    pallas_call x1, Pallas kernels, grad_call(): pl.pallas_call(functools.partial(grad_kernel, ndp, nt, nbytes), out_shape...  54.3 us
    pallas_call x1, Pallas kernels, byte_call(): pl.pallas_call(byte_kernel, out_shape=(jax.ShapeDtypeStruct(keys.shape, b...  9.71 us

profile of v2, /device:TPU:0, one launch (start us, length us, event | category | flops | bytes accessed | tf_op | source)
XLA Modules:
  0.0 64.6 jit_solution(13817458240338442600)
XLA Ops:
  0.6 54.3 %shard_map.138 = (f32[64,1024]{1,0:T(8,128)}, f32[2,32,1024]{2,1,0:T(8,128)}, bf16[2,384,128]{2,1,0:T(8,128)(2,1)}, bf16[2,384,128]{2,1,0:T(8,128)(2,1)}, s32[2,128]{1,0:T(2,128)}, /*index=5*/s32[2,896]{1,0:T(2,128)}) custom-call(bf16[384,1024]{1,0:T(8,128)(2,1)} %bitcast.15, bf16[384,1024]{1,0:T(8,128)(2,1)} %bitcast.16, bf16[384,512]{1,0:T(8,128)(2,1)} %bitcast.17, ...), custom_call_target="tpu_custom_call" | custom-call | tf_op jit(solution)/shard_map/pallas_call | solution.py:563
  54.9 9.7 %shard_map.139 = (bf16[8192,128]{1,0:T(8,128)(2,1)}, bf16[8192,128]{1,0:T(8,128)(2,1)}, f32[64,1024]{1,0:T(8,128)}, f32[64,1024]{1,0:T(8,128)}) custom-call(s32[2,128]{1,0:T(2,128)} %get-tuple-element.14.tab, s32[2,896]{1,0:T(2,128)} %get-tuple-element.15.bounds, bf16[768,128]{1,0:T(8,128)(2,1)} %bitcast.20, bf16[768,128]{1,0:T(8,128)(2,1)} %bitcast.21, ...), custom_call_target="tpu_custom_call" | custom-call | tf_op jit(solution)/shard_map/pallas_call | solution.py:762

commit v3 on v2

--- a/solution.py
+++ b/solution.py
@@ -157,15 +157,25 @@
 
 
 BLK = 256
+GROUP = 8
 WIN = 128
+
+
+def tile_terms(b, w, keys, values, bd, bounds):
+    both = jnp.concatenate([keys[b], values[b]], axis=1)
+    s = lax.dot_general(both, bd[w], (((1,), (1,)), ((), ())), preferred_element_type=jnp.float32)
+    row = lax.broadcasted_iota(jnp.int32, (BLK, WIN), 0) + b * BLK
+    limits = bounds[w]
+    inside = (row >= limits[0:1, :]) & (row < limits[1:2, :])
+    return jnp.where(inside, jnp.exp(s[:, :WIN] * (1.0 / math.sqrt(HD))), 0.0), s[:, WIN:]
 
 
 def grad_kernel(
     ndp, nt, nbytes, states_in, resid_in, up_in, gain_in, vw, ow, ctx_in, q_in, starts,
-    wgv, wgo, g_out, q_out, tab, bounds,
+    keys_in, values_in, wgv, wgo, bd_out, e_out, p_out, tab, table, means,
     states, resid, up, ctx, gain, wall, sqs, sqr, part, acc, acco, accz, rbz, lbz, ysz, yrz, rbv, lbv, ysv, yrv, rbo, lbo, yso, yro,
-    pas, par, gn, nrm, gpat, trans_v, trans_o, gsend, gboth, qboth,
-    s_in, s_own, s_out, s_ag, r_ag, s_sq, r_sq, s_rv, r_rv, s_lv, r_lv, s_ro, r_ro, s_lo, r_lo,
+    pas, par, gn, nrm, gpat, trans_v, trans_o, gsend, gboth, qboth, keys, values, bd, bounds, expo, pgrad, psums, tab_s,
+    s_in, s_e, s_p, s_out, s_ag, r_ag, s_sq, r_sq, s_rv, r_rv, s_lv, r_lv, s_ro, r_ro, s_lo, r_lo,
     s_rz, r_rz, s_lz, r_lz, s_yo, r_yo, s_yv, r_yv, s_pa, r_pa, s_g, r_g,
 ):
     dp, sq, tn = lax.axis_index("dp"), lax.axis_index("seq"), lax.axis_index("tensor")
@@ -193,7 +203,7 @@
     for i, (name, src, dst) in enumerate(
         (("states", states_in, states), ("up", up_in, up), ("resid", resid_in, resid),
          ("ctx", ctx_in, ctx), ("q", q_in, qboth.at[sq]), ("vw", vw, wall.at[0, mine]),
-         ("ow", ow, wall.at[1, mine]))
+         ("ow", ow, wall.at[1, mine]), ("keys", keys_in, keys), ("values", values_in, values))
     ):
         local[name] = pltpu.make_async_copy(src, dst, s_in.at[i])
         local[name].start()
@@ -393,20 +403,20 @@
     after = jnp.where(
         lane == first.shape[1] - 1, 2 * nbytes, pltpu.roll(row8, first.shape[1] - 1, 1)
     )
-    far = jnp.full((1, WIN), 4 * nbytes, jnp.int32)
-    bounds[0:1, : first.shape[1]] = first
-    bounds[1:2, : first.shape[1]] = after[0:1, :]
-    bounds[0:1, first.shape[1] :] = far
-    bounds[1:2, first.shape[1] :] = far
+    for w in range(first.shape[1] // WIN):
+        lanes = slice(w * WIN, (w + 1) * WIN)
+        bounds[w, 0:1, :] = first[:, lanes]
+        bounds[w, 1:2, :] = after[0:1, lanes]
+    bounds[first.shape[1] // WIN] = jnp.full(bounds.shape[1:], 4 * nbytes, jnp.int32)
 
     ag_forward(0, 1, 0)
+    for h in range(2):
+        ag_own_z(1, h, inner=False)
     for c in sq_copies:
         c.wait_recv()
     row_loop(normalise)
     ag_forward(0, 1, 1)
     wgrad(0, trans_v, nrm)
-    for h in range(2):
-        ag_own_z(1, h, inner=False)
     line_open(part_v, line_v)
     ag_forward(0, 2, 0)
     nblocks = nbytes // BLK
@@ -420,7 +430,16 @@
     window = lax.broadcasted_iota(jnp.int32, (1, 128), 1) - block_of + low
     done = block_of >= nblocks
     tab[0:1, :] = jnp.where(done, nblocks - 1, block_of)
-    tab[1:2, :] = jnp.where(done, first.shape[1] // WIN, window)
+    nwin = first.shape[1] // WIN
+    window = jnp.where(done, nwin, window)
+    tab[1:2, :] = window
+    window_of = jnp.broadcast_to(window.astype(jnp.float32), (128, 128)).T[: psums.shape[1], 0:1]
+    local["tab"] = pltpu.make_async_copy(tab, tab_s, s_in.at[9])
+    local["tab"].start()
+    for w in range(nwin):
+        bd[w, :WIN, HD:] = jnp.zeros((WIN, HD), jnp.bfloat16)
+        bd[w, WIN:, :HD] = jnp.zeros((WIN, HD), jnp.bfloat16)
+    bd[nwin] = jnp.zeros(bd.shape[1:], jnp.bfloat16)
 
     ag_forward(0, 2, 1)
     local["ctx"].wait()
@@ -522,41 +541,86 @@
         line_end(h, accz, line_z)
     ysz[...] = accz[1 - sq].astype(jnp.bfloat16)
     yz = go(copy(ysz, yrz, s_yv.at[1], r_yv.at[1], ydev))
+    ngroup = psums.shape[1] // GROUP
+
+    def terms(group):
+        here = pl.ds(group * GROUP, GROUP)
+        return (
+            pltpu.make_async_copy(expo.at[here], e_out.at[here], s_e.at[group]),
+            pltpu.make_async_copy(pgrad.at[here], p_out.at[here], s_p.at[group]),
+        )
+
+    def measure(group, _):
+        for k in range(GROUP):
+            n = group * GROUP + k
+            e, pg = tile_terms(tab_s[0, n], tab_s[1, n], keys, values, bd, bounds)
+            expo[n] = e.astype(jnp.bfloat16)
+            t = jnp.sum(e, axis=0, keepdims=True)
+            m = jnp.sum(e * pg, axis=0, keepdims=True)
+            mean = m / jnp.where(t > 0.0, t, 1.0)
+            pgrad[n] = (pg - mean).astype(jnp.bfloat16)
+            psums[0, pl.ds(n, 1), :] = t
+            psums[1, pl.ds(n, 1), :] = m
+            means[pl.ds(n, 1), :] = mean
+        for c in terms(group):
+            c.start()
+        return 0
+
     line(1, 0, part_o, line_o)
     yv.wait_recv()
     acc[0] = acc[sq] + yrv[...].astype(jnp.float32)
     out_v = pltpu.make_async_copy(acc.at[0], wgv, s_out.at[0])
     out_v.start()
+    qc.wait_recv()
+    for c in gc:
+        c.wait_recv()
+    for w in range(nwin):
+        at = (w * WIN // patches, pl.ds(w * WIN % patches, WIN))
+        bd[w, :WIN, :HD] = qboth[at]
+        bd[w, WIN:, HD:] = gboth[at]
+    out_bd = pltpu.make_async_copy(bd, bd_out, s_out.at[2])
+    out_bd.start()
+    for name in ("keys", "values", "tab"):
+        local[name].wait()
+    lax.fori_loop(0, ngroup, measure, 0)
+    for w in range(nwin):
+        lanes = slice(w * WIN, (w + 1) * WIN)
+        here = window_of == float(w)
+        t = jnp.sum(jnp.where(here, psums[0], 0.0), axis=0, keepdims=True)
+        m = jnp.sum(jnp.where(here, psums[1], 0.0), axis=0, keepdims=True)
+        inv = jnp.where(t > 0.0, 1.0 / jnp.where(t > 0.0, t, 1.0), 0.0)
+        table[0:1, lanes] = inv
+        table[1:2, lanes] = m * inv
+    table[:, nwin * WIN :] = jnp.zeros((2, WIN), jnp.float32)
     acco[0] = part_o(dp, 0)
     line_end(0, acco, line_o)
     yz.wait_recv()
     acco[1] = accz[sq] + yrz[...].astype(jnp.float32)
     out_o = pltpu.make_async_copy(acco, wgo, s_out.at[1])
     out_o.start()
-    qc.wait_recv()
-    for c in gc:
-        c.wait_recv()
-    out_q = pltpu.make_async_copy(qboth, q_out, s_out.at[2])
-    out_q.start()
-    out_g = pltpu.make_async_copy(gboth, g_out, s_out.at[3])
-    out_g.start()
+    for group in range(ngroup):
+        for c in terms(group):
+            c.wait()
     for c, cond in sent:
         if cond is None:
             c.wait_send()
         else:
             pl.when(cond)(c.wait_send)
-    for c in (out_v, out_o, out_q, out_g):
+    for c in (out_v, out_o, out_bd):
         c.wait()
 
 
-def grad_call(ndp, nt, nbytes, states, resid, up, gain, vw, ow, ctx, q, starts):
+def grad_call(ndp, nt, states, resid, up, gain, vw, ow, ctx, q, starts, keys, values):
     patches, width = states.shape
     rows = vw.shape[0]
     nblk = 2 * ndp
     nk = up.shape[1]
     bf, f32, i32 = jnp.bfloat16, jnp.float32, jnp.int32
     nrow = patches // 128
+    nbytes = keys.shape[0] * BLK
     total = starts.shape[1]
+    nwin = total // WIN
+    npair = -(-(nbytes // BLK + nwin - 1) // GROUP) * GROUP
     vmem = pl.BlockSpec(memory_space=pltpu.VMEM)
     hbm = pl.BlockSpec(memory_space=pl.ANY)
     dma = pltpu.SemaphoreType.DMA
@@ -565,13 +629,15 @@
         out_shape=(
             jax.ShapeDtypeStruct((rows, width), f32),
             jax.ShapeDtypeStruct((2, rows // 2, width), f32),
-            jax.ShapeDtypeStruct((2, patches, HD), bf),
-            jax.ShapeDtypeStruct((2, patches, HD), bf),
+            jax.ShapeDtypeStruct((nwin + 1, 2 * WIN, 2 * HD), bf),
+            jax.ShapeDtypeStruct((npair, BLK, WIN), bf),
+            jax.ShapeDtypeStruct((npair, BLK, WIN), bf),
             jax.ShapeDtypeStruct((2, 128), i32),
-            jax.ShapeDtypeStruct((2, total + WIN), i32),
+            jax.ShapeDtypeStruct((2, total + WIN), f32),
+            jax.ShapeDtypeStruct((npair, WIN), f32),
         ),
-        in_specs=[hbm, hbm, hbm, vmem, hbm, hbm, hbm, hbm, vmem],
-        out_specs=[hbm] * 4 + [vmem] * 2,
+        in_specs=[hbm, hbm, hbm, vmem, hbm, hbm, hbm, hbm, vmem, hbm, hbm],
+        out_specs=[hbm] * 5 + [vmem] * 3,
         scratch_shapes=[
             pltpu.VMEM((patches, width), bf),
             pltpu.VMEM((patches, width), bf),
@@ -607,7 +673,15 @@
             pltpu.VMEM((nt - 1, patches, HD), bf),
             pltpu.VMEM((2, patches, HD), bf),
             pltpu.VMEM((2, patches, HD), bf),
-            dma((7,)), dma((2,)), dma((4,)),
+            pltpu.VMEM(keys.shape, bf),
+            pltpu.VMEM(keys.shape, bf),
+            pltpu.VMEM((nwin + 1, 2 * WIN, 2 * HD), bf),
+            pltpu.VMEM((nwin + 1, 2, WIN), i32),
+            pltpu.VMEM((npair, BLK, WIN), bf),
+            pltpu.VMEM((npair, BLK, WIN), bf),
+            pltpu.VMEM((2, npair, WIN), f32),
+            pltpu.SMEM((2, 128), i32),
+            dma((10,)), dma((npair // GROUP,)), dma((npair // GROUP,)), dma((3,)),
             dma((2, 2, 6 * ndp)), dma((2, 2, nblk)),
             dma((2, nt - 1)), dma((2, nt - 1)),
             dma((ndp, 2)), dma((ndp, 2)), dma((ndp, 2)), dma((ndp, 2)),
@@ -619,43 +693,45 @@
         compiler_params=pltpu.CompilerParams(
             collective_id=0, has_side_effects=True, vmem_limit_bytes=60 * 1024 * 1024
         ),
-    )(states, resid, up, gain, vw, ow, ctx, q, starts)
-
-
-GROUP = 8
+    )(states, resid, up, gain, vw, ow, ctx, q, starts, keys, values)
 
 
 def byte_kernel(
-    tab, bounds, g, q, wgv_in, wgo_in, keys_in, values_in, gk_out, gv_out, wgv, wgo,
-    keys, values, gk, gv, expo, pgrad, bd, sums, table, held, s_k, s_v, o_k, o_v, s_w,
+    tab_in, table_in, means_in, bd_in, e_in, p_in, wgv_in, wgo_in, gk_out, gv_out, wgv, wgo,
+    tab, table, means, bd, expo, pgrad, gk, gv, held, s_e, s_p, o_k, o_v, s_w, s_t,
 ):
-    total = g.shape[0]
-    nwin = total // WIN
-    nbytes = keys.shape[0]
-    chunk = GROUP * BLK
-    nchunk = nbytes // chunk
-    lag = 1 + -(-(nwin - 1) // GROUP)
+    nwin = bd.shape[0] - 1
+    nbytes = gk.shape[0]
     ngroup = expo.shape[0] // GROUP
+    nchunk = o_k.shape[0]
+    chunk = nbytes // nchunk
+    ready = GROUP * BLK // chunk
+    behind = -(-(nwin - 1) // (chunk // BLK))
     scale = 1.0 / math.sqrt(HD)
 
-    def rows_of(c):
-        return pl.ds(pl.multiple_of(c * chunk, chunk), chunk)
-
     def load(c):
-        here = rows_of(c)
+        here = pl.ds(c * GROUP, GROUP)
         return (
-            pltpu.make_async_copy(keys_in.at[here], keys.at[here], s_k.at[c]),
-            pltpu.make_async_copy(values_in.at[here], values.at[here], s_v.at[c]),
+            pltpu.make_async_copy(e_in.at[here], expo.at[here], s_e.at[c]),
+            pltpu.make_async_copy(p_in.at[here], pgrad.at[here], s_p.at[c]),
         )
 
     def store(c):
-        here = rows_of(c)
+        here = pl.ds(pl.multiple_of(c * chunk, chunk), chunk)
         return (
             pltpu.make_async_copy(gk.at[here], gk_out.at[here], o_k.at[c]),
             pltpu.make_async_copy(gv.at[here], gv_out.at[here], o_v.at[c]),
         )
 
-    for c in range(nchunk):
+    small = [
+        pltpu.make_async_copy(a, b, s_t.at[i])
+        for i, (a, b) in enumerate((
+            (tab_in, tab), (table_in, table), (means_in, means), (bd_in, bd)
+        ))
+    ]
+    for x in small:
+        x.start()
+    for c in range(ngroup):
         for x in load(c):
             x.start()
     carried = ((wgv_in, wgv), (wgo_in, wgo))
@@ -663,67 +739,26 @@
     passed = [pltpu.make_async_copy(held.at[i], b, s_w.at[2 + i]) for i, (_, b) in enumerate(carried)]
     for x in taken:
         x.start()
-
-    zero = jnp.zeros((WIN, HD), jnp.bfloat16)
-    for w in range(nwin):
-        bd[w, :WIN, :HD] = q[w * WIN : (w + 1) * WIN, :]
-        bd[w, WIN:, HD:] = g[w * WIN : (w + 1) * WIN, :]
-        bd[w, :WIN, HD:] = zero
-        bd[w, WIN:, :HD] = zero
-    bd[nwin] = jnp.zeros((2 * WIN, 2 * HD), jnp.bfloat16)
-    sums[...] = jnp.zeros_like(sums)
-    row = lax.broadcasted_iota(jnp.int32, (BLK, WIN), 0)
-
-    def place(n):
-        b, w = tab[0, n], tab[1, n]
-        return (
-            b, w, pl.ds(pl.multiple_of(b * BLK, BLK), BLK), pl.ds(pl.multiple_of(w * WIN, WIN), WIN)
-        )
-
-    def measure(group, _):
-        @pl.when(group < nchunk)
-        def _():
-            for x in load(group):
-                x.wait()
-
-        for k in range(GROUP):
-            n = group * GROUP + k
-            b, w, here, lanes = place(n)
-            both = jnp.concatenate([keys[here, :], values[here, :]], axis=1)
-            s = lax.dot_general(
-                both, bd[w], (((1,), (1,)), ((), ())), preferred_element_type=jnp.float32
-            )
-            lo = bounds[0:1, lanes] - b * BLK
-            hi = bounds[1:2, lanes] - b * BLK
-            e = jnp.where((row >= lo) & (row < hi), jnp.exp(s[:, :WIN] * scale), 0.0)
-            pg = s[:, WIN:]
-            expo[n] = e
-            pgrad[n] = pg
-            sums[0:1, lanes] += jnp.sum(e, axis=0, keepdims=True)
-            sums[1:2, lanes] += jnp.sum(e * pg, axis=0, keepdims=True)
-        return 0
-
-    lax.fori_loop(0, ngroup, measure, 0)
-    for x, y in zip(taken, passed):
+    for x in small:
         x.wait()
-        y.start()
-    t = sums[0:1, :]
-    inv = jnp.where(t > 0.0, 1.0 / jnp.where(t > 0.0, t, 1.0), 0.0)
-    table[0:1, :] = inv
-    table[1:2, :] = sums[1:2, :] * inv
 
     def apply(group, _):
+        for x in load(group):
+            x.wait()
         first = group * GROUP
         prior = jnp.maximum(first - 1, 0)
         before = pl.ds(pl.multiple_of(tab[0, prior] * BLK, BLK), BLK)
         held_k, held_v = gk[before, :], gv[before, :]
         for k in range(GROUP):
             n = first + k
-            b, w, here, lanes = place(n)
+            b, w = tab[0, n], tab[1, n]
+            here = pl.ds(pl.multiple_of(b * BLK, BLK), BLK)
+            lanes = pl.ds(pl.multiple_of(w * WIN, WIN), WIN)
             same = tab[0, jnp.maximum(n - 1, 0)] == b
             same = same & (n > 0) if k == 0 else same
-            p = expo[n] * table[0:1, lanes]
-            sg = p * (pgrad[n] - table[1:2, lanes]) * scale
+            p = expo[n].astype(jnp.float32) * table[0:1, lanes]
+            shift = means[pl.ds(n, 1), :] - table[1:2, lanes]
+            sg = p * (pgrad[n].astype(jnp.float32) + shift) * scale
             both = jnp.concatenate([sg.astype(jnp.bfloat16), p.astype(jnp.bfloat16)], axis=1)
             out = jnp.dot(both, bd[w], preferred_element_type=jnp.float32).astype(jnp.bfloat16)
             held_k = out[:, :HD] + jnp.where(same, held_k, jnp.zeros_like(held_k))
@@ -731,15 +766,21 @@
             gk[here, :] = held_k
             gv[here, :] = held_v
 
-        @pl.when((group >= lag) & (group - lag < nchunk))
-        def _():
-            for x in store(group - lag):
-                x.start()
+        for r in range(ready):
+            done = group * ready + r - behind
+
+            @pl.when((done >= 0) & (done < nchunk))
+            def _(done=done):
+                for x in store(done):
+                    x.start()
 
         return 0
 
     lax.fori_loop(0, ngroup, apply, 0)
-    for c in range(max(ngroup - lag, 0), nchunk):
+    for x, y in zip(taken, passed):
+        x.wait()
+        y.start()
+    for c in range(max(ngroup * ready - behind, 0), nchunk):
         for x in store(c):
             x.start()
     for c in range(nchunk):
@@ -749,50 +790,45 @@
         x.wait()
 
 
-def byte_call(tab, bounds, g, q, wgv, wgo, keys, values):
+def byte_call(tab, table, means, bd, expo, pgrad, wgv, wgo, out):
     bf, f32 = jnp.bfloat16, jnp.float32
-    nbytes = keys.shape[0]
-    total = g.shape[0]
-    nwin = total // WIN
-    npair = -(-(nbytes // BLK + nwin - 1) // GROUP) * GROUP
-    nchunk = nbytes // (GROUP * BLK)
-    vmem = pl.BlockSpec(memory_space=pltpu.VMEM)
+    nchunk = out.shape[0] // 1024
+    ngroup = expo.shape[0] // GROUP
     hbm = pl.BlockSpec(memory_space=pl.ANY)
     dma = pltpu.SemaphoreType.DMA
     return pl.pallas_call(
         byte_kernel,
         out_shape=(
-            jax.ShapeDtypeStruct(keys.shape, bf),
-            jax.ShapeDtypeStruct(keys.shape, bf),
+            out,
+            out,
             jax.ShapeDtypeStruct(wgv.shape, f32),
             jax.ShapeDtypeStruct(wgo.shape, f32),
         ),
-        in_specs=[pl.BlockSpec(memory_space=pltpu.SMEM), vmem, vmem, vmem] + [hbm] * 4,
+        in_specs=[hbm] * 8,
         out_specs=[hbm] * 4,
         scratch_shapes=[
-            pltpu.VMEM(keys.shape, bf), pltpu.VMEM(keys.shape, bf),
-            pltpu.VMEM(keys.shape, bf), pltpu.VMEM(keys.shape, bf),
-            pltpu.VMEM((npair, BLK, WIN), f32), pltpu.VMEM((npair, BLK, WIN), f32),
-            pltpu.VMEM((nwin + 1, 2 * WIN, 2 * HD), bf),
-            pltpu.VMEM((8, total + WIN), f32), pltpu.VMEM((8, total + WIN), f32),
+            pltpu.SMEM(tab.shape, jnp.int32), pltpu.VMEM(table.shape, f32),
+            pltpu.VMEM(means.shape, f32), pltpu.VMEM(bd.shape, bf), pltpu.VMEM(expo.shape, bf), pltpu.VMEM(pgrad.shape, bf),
+            pltpu.VMEM(out.shape, bf), pltpu.VMEM(out.shape, bf),
             pltpu.VMEM((2,) + wgv.shape, f32),
-            dma((nchunk,)), dma((nchunk,)), dma((nchunk,)), dma((nchunk,)), dma((4,)),
+            dma((ngroup,)), dma((ngroup,)), dma((nchunk,)), dma((nchunk,)), dma((4,)), dma((4,)),
         ],
         compiler_params=pltpu.CompilerParams(vmem_limit_bytes=60 * 1024 * 1024),
-    )(tab, bounds, g, q, wgv, wgo, keys, values)
+    )(tab, table, means, bd, expo, pgrad, wgv, wgo)
 
 
 def on_device_kernels(
     ndp, nt, patch_states, residual_grad, upstream_value, norm_gain, value_weight, out_weight,
     attn_out, queries, byte_keys, byte_values, patch_starts,
 ):
-    nbytes = byte_keys.shape[1]
-    wgv, wgo, g, q, tab, bounds = grad_call(
-        ndp, nt, nbytes, patch_states[0], residual_grad[0], upstream_value[0],
+    wgv, wgo, bd, expo, pgrad, tab, table, means = grad_call(
+        ndp, nt, patch_states[0], residual_grad[0], upstream_value[0],
         norm_gain.reshape(-1, 128), value_weight, out_weight, attn_out[0], queries[0], patch_starts,
+        byte_keys.reshape(-1, BLK, HD), byte_values.reshape(-1, BLK, HD),
     )
     gk, gv, wgv, wgo = byte_call(
-        tab, bounds, g.reshape(-1, HD), q.reshape(-1, HD), wgv, wgo.reshape(wgv.shape), byte_keys[0], byte_values[0]
+        tab, table, means, bd, expo, pgrad, wgv, wgo.reshape(wgv.shape),
+        jax.ShapeDtypeStruct(byte_keys[0].shape, jnp.bfloat16),
     )
     return (wgv, wgo, gk[None], gv[None])
 

time: 64.8 us -> 61.2 us (0.944)
  Pallas kernels: 64 us -> 60.4 us
    pallas_call x1, Pallas kernels: 9.71 us -> 6.93 us  [byte_call(): pl.pallas_call(byte_kernel, out_shape=(out, out, jax.ShapeDtypeStruct(wgv...]
    pallas_call x1, Pallas kernels: 54.3 us -> 53.4 us  [grad_call(): pl.pallas_call(functools.partial(grad_kernel, ndp, nt, nbytes), out_shape...]
where the time goes in v3:
time: 61.2 us; the launch traced here: 61 us
  Pallas kernels  60.4 us (99%)
  between operations  0.64 us (1%)
    pallas_call x1, Pallas kernels, grad_call(): pl.pallas_call(functools.partial(grad_kernel, ndp, nt, nbytes), out_shape...  53.4 us
    pallas_call x1, Pallas kernels, byte_call(): pl.pallas_call(byte_kernel, out_shape=(out, out, jax.ShapeDtypeStruct(wgv...  6.93 us

profile of v3, /device:TPU:0, one launch (start us, length us, event | category | flops | bytes accessed | tf_op | source)
XLA Modules:
  0.0 61.0 jit_solution(3577410401091479693)
XLA Ops:
  0.6 53.4 %shard_map.138 = (f32[64,1024]{1,0:T(8,128)}, f32[2,32,1024]{2,1,0:T(8,128)}, bf16[7,256,256]{2,1,0:T(8,128)(2,1)}, bf16[40,256,128]{2,1,0:T(8,128)(2,1)}, bf16[...) custom-call(bf16[384,1024]{1,0:T(8,128)(2,1)} %bitcast.13, ...), custom_call_target="tpu_custom_call" | custom-call | tf_op jit(solution)/shard_map/pallas_call | solution.py:627
  54.1 6.9 %shard_map.139 = (bf16[8192,128]{1,0:T(8,128)(2,1)}, bf16[8192,128]{1,0:T(8,128)(2,1)}, f32[64,1024]{1,0:T(8,128)}, f32[64,1024]{1,0:T(8,128)}) custom-call(s32[2,128]{1,0:T(2,128)} %get-tuple-element.16.tab_in, f32[2,896]{1,0:T(2,128)} %get-tuple-element.17.table_in, f32[40,128]{1,0:T(8,128)} %get-tuple-element.18.means_in, ...), custom_call_target="tpu_custom_call" | custom-call | tf_op jit(solution)/shard_map/pallas_call | solution.py:799

commit v4 on v3

--- a/solution.py
+++ b/solution.py
@@ -161,20 +161,25 @@
 WIN = 128
 
 
-def tile_terms(b, w, keys, values, bd, bounds):
-    both = jnp.concatenate([keys[b], values[b]], axis=1)
-    s = lax.dot_general(both, bd[w], (((1,), (1,)), ((), ())), preferred_element_type=jnp.float32)
+def tile_scores(b, w, keys, qb, bounds):
+    s = lax.dot_general(keys[b], qb[w], (((1,), (1,)), ((), ())), preferred_element_type=jnp.float32)
     row = lax.broadcasted_iota(jnp.int32, (BLK, WIN), 0) + b * BLK
     limits = bounds[w]
     inside = (row >= limits[0:1, :]) & (row < limits[1:2, :])
-    return jnp.where(inside, jnp.exp(s[:, :WIN] * (1.0 / math.sqrt(HD))), 0.0), s[:, WIN:]
+    return jnp.where(inside, jnp.exp(s * (1.0 / math.sqrt(HD))), 0.0)
+
+
+def tile_products(b, w, values, gb):
+    return lax.dot_general(
+        values[b], gb[w], (((1,), (1,)), ((), ())), preferred_element_type=jnp.float32
+    )
 
 
 def grad_kernel(
     ndp, nt, nbytes, states_in, resid_in, up_in, gain_in, vw, ow, ctx_in, q_in, starts,
     keys_in, values_in, wgv, wgo, bd_out, e_out, p_out, tab, table, means,
     states, resid, up, ctx, gain, wall, sqs, sqr, part, acc, acco, accz, rbz, lbz, ysz, yrz, rbv, lbv, ysv, yrv, rbo, lbo, yso, yro,
-    pas, par, gn, nrm, gpat, trans_v, trans_o, gsend, gboth, qboth, keys, values, bd, bounds, expo, pgrad, psums, tab_s,
+    pas, par, gn, nrm, gpat, trans_v, trans_o, gsend, gboth, qboth, keys, values, bd, qb, gb, bounds, expo, pgrad, psums, tab_s,
     s_in, s_e, s_p, s_out, s_ag, r_ag, s_sq, r_sq, s_rv, r_rv, s_lv, r_lv, s_ro, r_ro, s_lo, r_lo,
     s_rz, r_rz, s_lz, r_lz, s_yo, r_yo, s_yv, r_yv, s_pa, r_pa, s_g, r_g,
 ):
@@ -440,6 +445,8 @@
         bd[w, :WIN, HD:] = jnp.zeros((WIN, HD), jnp.bfloat16)
         bd[w, WIN:, :HD] = jnp.zeros((WIN, HD), jnp.bfloat16)
     bd[nwin] = jnp.zeros(bd.shape[1:], jnp.bfloat16)
+    qb[nwin] = jnp.zeros((WIN, HD), jnp.bfloat16)
+    gb[nwin] = jnp.zeros((WIN, HD), jnp.bfloat16)
 
     ag_forward(0, 2, 1)
     local["ctx"].wait()
@@ -448,6 +455,7 @@
         ag_forward(0, 3, h)
         ag_own_z(1, h, ends=False)
         ag_own_y(1, h)
+    line(2, 0, part_v, line_v)
     ag_forward(1, 1, 0)
     local["vw"].wait()
     ag_wait_y(0)
@@ -462,12 +470,11 @@
 
     row_loop(project)
     cr_copies = share(1)
+    line(2, 1, part_v, line_v)
     ag_cross(1, 0)
     ag_forward(1, 2, 0)
     ag_cross(1, 1)
-    line(2, 0, part_v, line_v)
     ag_forward(1, 2, 1)
-    line(2, 1, part_v, line_v)
     local["resid"].wait()
     for c in cr_copies:
         c.wait_recv()
@@ -523,6 +530,66 @@
         line_end(h, acc, line_v)
     ysv[...] = acc[1 - sq].astype(jnp.bfloat16)
     yv = go(copy(ysv, yrv, s_yv.at[0], r_yv.at[0], ydev))
+    ngroup = psums.shape[1] // GROUP
+
+    def e_copy(group):
+        here = pl.ds(group * GROUP, GROUP)
+        return pltpu.make_async_copy(expo.at[here], e_out.at[here], s_e.at[group])
+
+    def p_copy(group):
+        here = pl.ds(group * GROUP, GROUP)
+        return pltpu.make_async_copy(pgrad.at[here], p_out.at[here], s_p.at[group])
+
+    def scores(group, _):
+        for k in range(GROUP):
+            n = group * GROUP + k
+            e = tile_scores(tab_s[0, n], tab_s[1, n], keys, qb, bounds).astype(jnp.bfloat16)
+            expo[n] = e
+            psums[0, pl.ds(n, 1), :] = jnp.sum(e.astype(jnp.float32), axis=0, keepdims=True)
+        e_copy(group).start()
+        return 0
+
+    def products(group, _):
+        for k in range(GROUP):
+            n = group * GROUP + k
+            pg = tile_products(tab_s[0, n], tab_s[1, n], values, gb)
+            t = psums[0, pl.ds(n, 1), :]
+            m = jnp.sum(expo[n].astype(jnp.float32) * pg, axis=0, keepdims=True)
+            mean = m / jnp.where(t > 0.0, t, 1.0)
+            pgrad[n] = (pg - mean).astype(jnp.bfloat16)
+            psums[1, pl.ds(n, 1), :] = m
+            means[pl.ds(n, 1), :] = mean
+        p_copy(group).start()
+        return 0
+
+    def window_rows(w):
+        return (w * WIN // patches, pl.ds(w * WIN % patches, WIN))
+
+    def window_total(which, w):
+        return jnp.sum(
+            jnp.where(window_of == float(w), psums[which], 0.0), axis=0, keepdims=True
+        )
+
+    def open_scores():
+        qc.wait_recv()
+        for name in ("keys", "values", "tab"):
+            local[name].wait()
+        for w in range(nwin):
+            rows = qboth[window_rows(w)]
+            qb[w] = rows
+            bd[w, :WIN, :HD] = rows
+
+    def close_scores():
+        for w in range(nwin):
+            t = window_total(0, w)
+            table[0:1, w * WIN : (w + 1) * WIN] = jnp.where(
+                t > 0.0, 1.0 / jnp.where(t > 0.0, t, 1.0), 0.0
+            )
+        table[:, nwin * WIN :] = jnp.zeros((2, WIN), jnp.float32)
+
+    open_scores()
+    lax.fori_loop(0, ngroup, scores, 0)
+    close_scores()
     line_open(part_o, line_o, (0,))
     for h in range(2):
         line(1, h, part_z, line_z)
@@ -541,57 +608,23 @@
         line_end(h, accz, line_z)
     ysz[...] = accz[1 - sq].astype(jnp.bfloat16)
     yz = go(copy(ysz, yrz, s_yv.at[1], r_yv.at[1], ydev))
-    ngroup = psums.shape[1] // GROUP
-
-    def terms(group):
-        here = pl.ds(group * GROUP, GROUP)
-        return (
-            pltpu.make_async_copy(expo.at[here], e_out.at[here], s_e.at[group]),
-            pltpu.make_async_copy(pgrad.at[here], p_out.at[here], s_p.at[group]),
-        )
-
-    def measure(group, _):
-        for k in range(GROUP):
-            n = group * GROUP + k
-            e, pg = tile_terms(tab_s[0, n], tab_s[1, n], keys, values, bd, bounds)
-            expo[n] = e.astype(jnp.bfloat16)
-            t = jnp.sum(e, axis=0, keepdims=True)
-            m = jnp.sum(e * pg, axis=0, keepdims=True)
-            mean = m / jnp.where(t > 0.0, t, 1.0)
-            pgrad[n] = (pg - mean).astype(jnp.bfloat16)
-            psums[0, pl.ds(n, 1), :] = t
-            psums[1, pl.ds(n, 1), :] = m
-            means[pl.ds(n, 1), :] = mean
-        for c in terms(group):
-            c.start()
-        return 0
-
     line(1, 0, part_o, line_o)
     yv.wait_recv()
     acc[0] = acc[sq] + yrv[...].astype(jnp.float32)
     out_v = pltpu.make_async_copy(acc.at[0], wgv, s_out.at[0])
     out_v.start()
-    qc.wait_recv()
     for c in gc:
         c.wait_recv()
     for w in range(nwin):
-        at = (w * WIN // patches, pl.ds(w * WIN % patches, WIN))
-        bd[w, :WIN, :HD] = qboth[at]
-        bd[w, WIN:, HD:] = gboth[at]
+        rows = gboth[window_rows(w)]
+        gb[w] = rows
+        bd[w, WIN:, HD:] = rows
     out_bd = pltpu.make_async_copy(bd, bd_out, s_out.at[2])
     out_bd.start()
-    for name in ("keys", "values", "tab"):
-        local[name].wait()
-    lax.fori_loop(0, ngroup, measure, 0)
+    lax.fori_loop(0, ngroup, products, 0)
     for w in range(nwin):
         lanes = slice(w * WIN, (w + 1) * WIN)
-        here = window_of == float(w)
-        t = jnp.sum(jnp.where(here, psums[0], 0.0), axis=0, keepdims=True)
-        m = jnp.sum(jnp.where(here, psums[1], 0.0), axis=0, keepdims=True)
-        inv = jnp.where(t > 0.0, 1.0 / jnp.where(t > 0.0, t, 1.0), 0.0)
-        table[0:1, lanes] = inv
-        table[1:2, lanes] = m * inv
-    table[:, nwin * WIN :] = jnp.zeros((2, WIN), jnp.float32)
+        table[1:2, lanes] = window_total(1, w) * table[0:1, lanes]
     acco[0] = part_o(dp, 0)
     line_end(0, acco, line_o)
     yz.wait_recv()
@@ -599,8 +632,8 @@
     out_o = pltpu.make_async_copy(acco, wgo, s_out.at[1])
     out_o.start()
     for group in range(ngroup):
-        for c in terms(group):
-            c.wait()
+        e_copy(group).wait()
+        p_copy(group).wait()
     for c, cond in sent:
         if cond is None:
             c.wait_send()
@@ -676,6 +709,8 @@
             pltpu.VMEM(keys.shape, bf),
             pltpu.VMEM(keys.shape, bf),
             pltpu.VMEM((nwin + 1, 2 * WIN, 2 * HD), bf),
+            pltpu.VMEM((nwin + 1, WIN, HD), bf),
+            pltpu.VMEM((nwin + 1, WIN, HD), bf),
             pltpu.VMEM((nwin + 1, 2, WIN), i32),
             pltpu.VMEM((npair, BLK, WIN), bf),
             pltpu.VMEM((npair, BLK, WIN), bf),
@@ -776,10 +811,11 @@
 
         return 0
 
-    lax.fori_loop(0, ngroup, apply, 0)
+    lax.fori_loop(0, 1, apply, 0)
     for x, y in zip(taken, passed):
         x.wait()
         y.start()
+    lax.fori_loop(1, ngroup, apply, 0)
     for c in range(max(ngroup * ready - behind, 0), nchunk):
         for x in store(c):
             x.start()
@@ -792,7 +828,7 @@
 
 def byte_call(tab, table, means, bd, expo, pgrad, wgv, wgo, out):
     bf, f32 = jnp.bfloat16, jnp.float32
-    nchunk = out.shape[0] // 1024
+    nchunk = out.shape[0] // 2048
     ngroup = expo.shape[0] // GROUP
     hbm = pl.BlockSpec(memory_space=pl.ANY)
     dma = pltpu.SemaphoreType.DMA

time: 61.2 us -> 60.2 us (0.984)
  Pallas kernels: 60.4 us -> 59.3 us
    pallas_call x1, Pallas kernels: 53.4 us -> 52.6 us  [grad_call(): pl.pallas_call(functools.partial(grad_kernel, ndp, nt, nbytes), out_shape...]
where the time goes in v4:
time: 60.2 us; the launch traced here: 60 us
  Pallas kernels  59.3 us (99%)
  between operations  0.64 us (1%)
    pallas_call x1, Pallas kernels, grad_call(): pl.pallas_call(functools.partial(grad_kernel, ndp, nt, nbytes), out_shape...  52.6 us
    pallas_call x1, Pallas kernels, byte_call(): pl.pallas_call(byte_kernel, out_shape=(out, out, jax.ShapeDtypeStruct(wgv...  6.72 us

profile of v4, /device:TPU:0, one launch (start us, length us, event | category | flops | bytes accessed | tf_op | source)
XLA Modules:
  0.0 60.0 jit_solution(14769166699207398697)
XLA Ops:
  0.6 52.6 %shard_map.138 = (f32[64,1024]{1,0:T(8,128)}, f32[2,32,1024]{2,1,0:T(8,128)}, bf16[7,256,256]{2,1,0:T(8,128)(2,1)}, bf16[40,256,128]{2,1,0:T(8,128)(2,1)}, bf16[...) custom-call(bf16[384,1024]{1,0:T(8,128)(2,1)} %bitcast.13, ...), custom_call_target="tpu_custom_call" | custom-call | tf_op jit(solution)/shard_map/pallas_call | solution.py:660
  53.3 6.7 %shard_map.139 = (bf16[8192,128]{1,0:T(8,128)(2,1)}, bf16[8192,128]{1,0:T(8,128)(2,1)}, f32[64,1024]{1,0:T(8,128)}, f32[64,1024]{1,0:T(8,128)}) custom-call(s32[2,128]{1,0:T(2,128)} %get-tuple-element.16.tab_in, f32[2,896]{1,0:T(2,128)} %get-tuple-element.17.table_in, f32[40,128]{1,0:T(8,128)} %get-tuple-element.18.means_in, ...), custom_call_target="tpu_custom_call" | custom-call | tf_op jit(solution)/shard_map/pallas_call | solution.py:835

commit v5 on v4

--- a/solution.py
+++ b/solution.py
@@ -609,10 +609,6 @@
     ysz[...] = accz[1 - sq].astype(jnp.bfloat16)
     yz = go(copy(ysz, yrz, s_yv.at[1], r_yv.at[1], ydev))
     line(1, 0, part_o, line_o)
-    yv.wait_recv()
-    acc[0] = acc[sq] + yrv[...].astype(jnp.float32)
-    out_v = pltpu.make_async_copy(acc.at[0], wgv, s_out.at[0])
-    out_v.start()
     for c in gc:
         c.wait_recv()
     for w in range(nwin):
@@ -622,6 +618,10 @@
     out_bd = pltpu.make_async_copy(bd, bd_out, s_out.at[2])
     out_bd.start()
     lax.fori_loop(0, ngroup, products, 0)
+    yv.wait_recv()
+    acc[0] = acc[sq] + yrv[...].astype(jnp.float32)
+    out_v = pltpu.make_async_copy(acc.at[0], wgv, s_out.at[0])
+    out_v.start()
     for w in range(nwin):
         lanes = slice(w * WIN, (w + 1) * WIN)
         table[1:2, lanes] = window_total(1, w) * table[0:1, lanes]

time: 60.2 us -> 60.2 us (level)
  no operation moved by 1% of the time
where the time goes in v5:
time: 60.2 us; the launch traced here: 60 us
  Pallas kernels  59.3 us (99%)
  between operations  0.64 us (1%)
    pallas_call x1, Pallas kernels, grad_call(): pl.pallas_call(functools.partial(grad_kernel, ndp, nt, nbytes), out_shape...  52.6 us
    pallas_call x1, Pallas kernels, byte_call(): pl.pallas_call(byte_kernel, out_shape=(out, out, jax.ShapeDtypeStruct(wgv...  6.71 us

profile of v5, /device:TPU:0, one launch (start us, length us, event | category | flops | bytes accessed | tf_op | source)
XLA Modules:
  0.0 60.0 jit_solution(17723652938834210967)
XLA Ops:
  0.6 52.6 %shard_map.138 = (f32[64,1024]{1,0:T(8,128)}, f32[2,32,1024]{2,1,0:T(8,128)}, bf16[7,256,256]{2,1,0:T(8,128)(2,1)}, bf16[40,256,128]{2,1,0:T(8,128)(2,1)}, bf16[...) custom-call(bf16[384,1024]{1,0:T(8,128)(2,1)} %bitcast.13, ...), custom_call_target="tpu_custom_call" | custom-call | tf_op jit(solution)/shard_map/pallas_call | solution.py:660
  53.3 6.7 %shard_map.139 = (bf16[8192,128]{1,0:T(8,128)(2,1)}, bf16[8192,128]{1,0:T(8,128)(2,1)}, f32[64,1024]{1,0:T(8,128)}, f32[64,1024]{1,0:T(8,128)}) custom-call(s32[2,128]{1,0:T(2,128)} %get-tuple-element.16.tab_in, f32[2,896]{1,0:T(2,128)} %get-tuple-element.17.table_in, f32[40,128]{1,0:T(8,128)} %get-tuple-element.18.means_in, ...), custom_call_target="tpu_custom_call" | custom-call | tf_op jit(solution)/shard_map/pallas_call | solution.py:835
